TPU v7x, 512 devices: a whole 4x8x8 slice. The times are simulated.
512 devices in a mesh: lat: 64 (over z, y), rad: 8 (over x, core).
Axes of the slice: x: 4, y: 8, z: 8, core: 2. Of those that a mesh axis runs over, the one named last changes fastest.
Arguments:
- tracer_values: float32 [64, 8, 3, 49152], P('lat', 'rad'), may hold values from 0 to 1
- tracer_cell: int32 [64, 8, 49152], P('lat', 'rad'), may hold values from 0 to 18431, as said below
- tracer_count: int32 [64, 8, 3], P('lat', 'rad'), may hold values from 2048 to 16384, as said below
- base_viscosity: float32 [768, 96, 128], P('lat', 'rad'), may hold values from 0.3 to 3
- velocity: float32 [3, 768, 96, 128], P(None, 'lat', 'rad'), may hold values from -6 to 6
- forcing: float32 [3, 768, 96, 128], P(None, 'lat', 'rad'), may hold values from -4 to 4
Outputs:
- smoothed: float32 [3, 768, 96, 128], P(None, 'lat', 'rad')
- composition: float32 [2, 768, 96, 128], P(None, 'lat', 'rad')
Inputs may be any that keep to these rules, and one draw needn't show every extreme that they name: `tracer_count`: in group g of a device (0: going to the device one lower along lat, 1: staying, 2: going to the device one higher) slots 0 to count - 1 hold tracers and the rest are empty; for every group some device has all 16384 slots in use (used slots, live or not). `tracer_cell`: index ((x * 12) + r) * 128 + y of a cell in the block of the device the tracer goes to, at the same rad index; tracers of slots below 16384 land in the last 2 x-planes of their device, tracers of slots from 32768 on in the first 2 x-planes.
All inputs are finite; a program needn't handle non-finite values.
Results may differ from a plain program's by a relative error of at most 0.0003.
The roundings to bfloat16 on the way count: a program that leaves them out, or rounds other values in their place, can miss the bound.
Values sent between devices are 32-bit elements; how exact they have to be, the bound alone decides.
A program may use at most 64 MiB of HBM per device.

v0:
```python
import jax
import jax.numpy as jnp
from jax import lax
from jax.sharding import PartitionSpec as P

SWEEPS = 2


LATERAL = 0.015625
RADIAL = 32.0
BUOYANCY = 0.1
PRIOR_WEIGHT = 0.5
CONTRAST_BASALT = 2.3
CONTRAST_MELT = 1.5


def extended(block, sides, width):
    for axis, dim in sides:
        count = lax.axis_size(axis)
        forward = [(i, i + 1) for i in range(count - 1)]
        backward = [(target, source) for source, target in forward]
        low = lax.ppermute(
            lax.slice_in_dim(block, block.shape[dim] - width, None, axis=dim), axis, forward
        )
        high = lax.ppermute(lax.slice_in_dim(block, 0, width, axis=dim), axis, backward)
        block = jnp.concatenate([low, block, high], axis=dim)
    return block


def plane_sums(
    tracer_loads, tracer_cells, plane_base, plane_count, lane_count, block_total, block_rows
):

    def accumulate(block_index, running):
        first_row = block_index * block_rows
        cell_block = lax.dynamic_slice_in_dim(tracer_cells, first_row, block_rows, 0)
        load_block = lax.dynamic_slice_in_dim(tracer_loads, first_row, block_rows, 1)
        plane_index = cell_block // lane_count - plane_base
        lane_index = cell_block % lane_count
        plane_hot = (
            plane_index[:, None] == jnp.arange(plane_count, dtype=jnp.int32)[None, :]
        ).astype(jnp.bfloat16)
        lane_hot = (lane_index[:, None] == jnp.arange(lane_count, dtype=jnp.int32)[None, :]).astype(
            jnp.bfloat16
        )
        spread = load_block[:, :, None] * lane_hot[None, :, :]
        product = lax.dot_general(
            plane_hot, spread, (((0,), (1,)), ((), ())), preferred_element_type=jnp.float32
        )
        return running + product.reshape(plane_count, 3 * lane_count)

    initial = jnp.zeros((plane_count, 3 * lane_count), jnp.float32)
    return lax.fori_loop(0, block_total, accumulate, initial)


def block_factor(diagonal, lower_band, upper_band):
    pivots = []
    upper_scaled = []
    for row_index in range(diagonal.shape[1]):
        if row_index == 0:
            pivot_row = diagonal[:, 0]
        else:
            pivot_row = diagonal[:, row_index] - lower_band[:, row_index] * upper_scaled[-1]
        pivots.append(pivot_row)
        upper_scaled.append(upper_band[:, row_index] / pivot_row)
    return (pivots, upper_scaled)


def block_solve(pivots, upper_scaled, lower_band, right_side):
    row_total = len(pivots)
    modified = []
    for row_index in range(row_total):
        if row_index == 0:
            value_row = right_side[:, :, 0] / pivots[0]
        else:
            value_row = (
                right_side[:, :, row_index] - lower_band[:, row_index] * modified[-1]
            ) / pivots[row_index]
        modified.append(value_row)
    solved = [modified[-1]]
    for row_index in range(row_total - 2, -1, -1):
        solved.append(modified[row_index] - upper_scaled[row_index] * solved[-1])
    ordered = solved[::-1]
    return jnp.stack(ordered, 2)


def interface_solve(coefficients):
    column_total = coefficients.shape[2]

    def forward(carried, inputs):
        offset, carried_slope = carried
        left_first, right_first, left_last, right_last, free_first, free_last = inputs
        divisor = 1.0 - left_first * carried_slope
        first_fixed = (free_first + left_first * offset) / divisor
        first_slope = right_first / divisor
        next_offset = free_last + left_last * (offset + carried_slope * first_fixed)
        next_slope = left_last * carried_slope * first_slope + right_last
        return ((next_offset, next_slope), (first_fixed, first_slope, next_offset, next_slope))

    start_state = (
        jnp.zeros((3, column_total), jnp.float32),
        jnp.zeros((column_total,), jnp.float32),
    )
    scan_inputs = (
        coefficients[:, 0],
        coefficients[:, 1],
        coefficients[:, 2],
        coefficients[:, 3],
        coefficients[:, 4:7],
        coefficients[:, 7:10],
    )
    final_state, eliminated = lax.scan(forward, start_state, scan_inputs)

    def backward(first_next, inputs):
        fixed_first, slope_first, fixed_last, slope_last = inputs
        first_value = fixed_first + slope_first * first_next
        last_value = fixed_last + slope_last * first_next
        return (first_value, (first_value, last_value))

    final_first, values_pair = lax.scan(
        backward, jnp.zeros((3, column_total), jnp.float32), eliminated, reverse=True
    )
    first_values, last_values = values_pair
    nothing_row = jnp.zeros((1, 3, column_total), jnp.float32)
    from_below = jnp.concatenate([nothing_row, last_values[:-1]], 0)
    from_above = jnp.concatenate([first_values[1:], nothing_row], 0)
    return jnp.concatenate([from_below, from_above], 1)


def reduced_boundary(interface):
    spread_columns = lax.all_to_all(interface, "rad", split_axis=2, concat_axis=0, tiled=True)
    solved = interface_solve(spread_columns)
    return lax.all_to_all(solved, "rad", split_axis=0, concat_axis=2, tiled=True)[0]


def local(tracer_values, tracer_cell, tracer_count, base_viscosity, velocity, forcing):
    cells_lateral, cells_radial, cells_side = base_viscosity.shape
    plane_total = cells_lateral * cells_radial
    slot_total = tracer_cell.shape[2]
    group_slots = slot_total // 3
    block_rows = min(2048, group_slots)
    values = tracer_values[0, 0]
    cells_flat = tracer_cell[0, 0]
    counts = tracer_count[0, 0]
    slot_index = jnp.arange(slot_total, dtype=jnp.int32)
    group_index = slot_index // group_slots
    within = slot_index - group_index * group_slots
    count_slot = jnp.where(
        group_index == 0, counts[0], jnp.where(group_index == 1, counts[1], counts[2])
    )
    weight = jnp.where(within < count_slot, 0.5 + values[0], jnp.float32(0.0))
    tracer_loads = jnp.stack([weight, weight * values[1], weight * values[2]]).astype(jnp.bfloat16)
    stay_blocks = group_slots // block_rows
    totals = plane_sums(
        tracer_loads[:, group_slots : 2 * group_slots],
        cells_flat[group_slots : 2 * group_slots],
        0,
        plane_total,
        cells_side,
        stay_blocks,
        block_rows,
    )
    payload = jnp.concatenate(
        [tracer_loads.astype(jnp.float32), cells_flat.astype(jnp.float32)[None, :]], 0
    )
    arrived = extended(payload, (("lat", 1),), group_slots)
    incoming_loads = jnp.concatenate(
        [arrived[:3, :group_slots], arrived[:3, 4 * group_slots :]], 1
    ).astype(jnp.bfloat16)
    incoming_cells = jnp.concatenate(
        [arrived[3, :group_slots], arrived[3, 4 * group_slots :]], 0
    ).astype(jnp.int32)
    totals = totals + plane_sums(
        incoming_loads,
        incoming_cells,
        0,
        plane_total,
        cells_side,
        2 * group_slots // block_rows,
        block_rows,
    )
    grouped = totals.reshape(cells_lateral, cells_radial, 3, cells_side)
    total_weight = grouped[:, :, 0] + PRIOR_WEIGHT
    basalt_share = grouped[:, :, 1] / total_weight
    melt_share = grouped[:, :, 2] / total_weight
    viscosity = base_viscosity * jnp.exp(
        CONTRAST_BASALT * basalt_share - CONTRAST_MELT * melt_share
    )
    viscosity_pad = extended(viscosity, (("lat", 0), ("rad", 1)), 1)
    side_pad = jnp.pad(viscosity, ((0, 0), (0, 0), (1, 1)))
    face_west = LATERAL * 0.5 * (viscosity + viscosity_pad[:-2, 1:-1])
    face_east = LATERAL * 0.5 * (viscosity + viscosity_pad[2:, 1:-1])
    face_south = LATERAL * 0.5 * (viscosity + side_pad[:, :, :-2])
    face_north = LATERAL * 0.5 * (viscosity + side_pad[:, :, 2:])
    face_below = RADIAL * 0.5 * (viscosity + viscosity_pad[1:-1, :-2])
    face_above = RADIAL * 0.5 * (viscosity + viscosity_pad[1:-1, 2:])
    diagonal = face_west + face_east + face_south + face_north + face_below + face_above
    source = jnp.concatenate([forcing[:2], (forcing[2] - BUOYANCY * basalt_share)[None]], 0)
    lower_band = -face_below
    upper_band = -face_above
    pivots, upper_scaled = block_factor(diagonal, lower_band, upper_band)
    radial_iota = lax.broadcasted_iota(jnp.int32, viscosity.shape, 1)
    response_side = jnp.stack(
        [
            jnp.where(radial_iota == 0, face_below, jnp.float32(0.0)),
            jnp.where(radial_iota == cells_radial - 1, face_above, jnp.float32(0.0)),
        ]
    )
    response = block_solve(pivots, upper_scaled, lower_band, response_side)
    current = velocity
    for sweep_index in range(SWEEPS):
        velocity_pad = extended(current, (("lat", 1),), 1)
        side_velocity = jnp.pad(current, ((0, 0), (0, 0), (0, 0), (1, 1)))
        right_side = (
            source
            + face_west * velocity_pad[:, :-2]
            + face_east * velocity_pad[:, 2:]
            + face_south * side_velocity[..., :-2]
            + face_north * side_velocity[..., 2:]
        )
        particular = block_solve(pivots, upper_scaled, lower_band, right_side)
        interface = jnp.concatenate(
            [response[:, :, 0], response[:, :, -1], particular[:, :, 0], particular[:, :, -1]], 0
        )
        interface = interface.reshape(1, 10, cells_lateral * cells_side)
        boundary = reduced_boundary(interface).reshape(6, cells_lateral, 1, cells_side)
        current = particular + response[0][None] * boundary[:3] + response[1][None] * boundary[3:]
    composition = jnp.stack([basalt_share, melt_share])
    return (current, composition)


def solution(mesh):
    return jax.shard_map(
        local,
        mesh=mesh,
        in_specs=(
            P("lat", "rad", None, None),
            P("lat", "rad", None),
            P("lat", "rad", None),
            P("lat", "rad", None),
            P(None, "lat", "rad", None),
            P(None, "lat", "rad", None),
        ),
        out_specs=(P(None, "lat", "rad", None), P(None, "lat", "rad", None)),
        check_vma=False,
    )
```

profile of v0, /device:TPU:248, one launch (start us, length us, event | category | flops | bytes accessed | tf_op | source)
XLA Modules:
  0.0 166.2 jit_solution(8829436223304811810)
XLA Ops:
  2.0 3.3 %fusion.121 = (bf16[1,49152]{1,0:T(2,128)(2,1)S(1)}, f32[1,49152]{1,0:T(1,128)S(1)}) fusion(f32[1,1,3,49152]{3,1,2,0:T(1,128)} %param.18, s32[]{:T(128)} %bitcast.3, s32[]{:T(128)} %bitcast.2, s32[]{:T(128)} %bitcast.1), kind=kLoop, calls=%fused_computation.411 | loop fusion | flops 884736 | bytes 491532 | tf_op jit(solution)/shard_map/convert.4
  6.8 3.3 %collective-permute-start.1 = (f32[4,16384]{1,0:T(4,128)S(1)}, f32[4,16384]{1,0:T(4,128)S(1)}, u32[]{:S(2)}, u32[]{:S(2)}) collective-permute-start(f32[4,16384]{1,0:T(4,128)S(1)} %get-tuple-element.1278), channel_id=1, source_target_pairs={{8,0},{16,8},{24,16},{32,24},{40,32},{48,40},{56,48},{64,56},{72,6... | collective-permute-start | bytes 786440 | tf_op jit(solution)/shard_map/ppermute | solution.py:25
  10.1 5.9 %collective-permute-start = (f32[4,16384]{1,0:T(4,128)S(1)}, f32[4,16384]{1,0:T(4,128)S(1)}, u32[]{:S(2)}, u32[]{:S(2)}) collective-permute-start(f32[4,16384]{1,0:T(4,128)S(1)} %get-tuple-element.1277), channel_id=1, source_target_pairs={{0,8},{8,16},{16,24},{24,32},{32,40},{40,48},{48,56},{56,64},{64,7... | collective-permute-start | bytes 786440 | tf_op jit(solution)/shard_map/ppermute | solution.py:22
  16.0 1.9 %collective-permute-start.3 = (f32[3,1,12,128]{3,2,1,0:T(8,128)S(1)}, f32[3,1,12,128]{3,2,1,0:T(8,128)S(1)}, u32[]{:S(2)}, u32[]{:S(2)}) collective-permute-start(f32[3,1,12,128]{3,2,1,0:T(8,128)S(1)} %get-tuple-element.1283), channel_id=1, source_target_pairs={{0,8},{8,16},{16,24},{24,32},{32,40},{40,48},{48,56},{56,64},{64,7... | collective-permute-start | bytes 55304 | tf_op jit(solution)/shard_map/ppermute | solution.py:22
  18.0 3.9 %collective-permute-start.5 = (f32[3,1,12,128]{3,2,1,0:T(8,128)S(1)}, f32[3,1,12,128]{3,2,1,0:T(8,128)S(1)}, u32[]{:S(2)}, u32[]{:S(2)}) collective-permute-start(f32[3,1,12,128]{3,2,1,0:T(8,128)S(1)} %get-tuple-element.1284), channel_id=1, source_target_pairs={{8,0},{16,8},{24,16},{32,24},{40,32},{48,40},{56,48},{64,56},{72,6... | collective-permute-start | bytes 55304 | tf_op jit(solution)/shard_map/ppermute | solution.py:25
  22.0 12.9 %while.112 = (s32[]{:T(128)}, f32[144,384]{1,0:T(8,128)S(1)}, s32[16384]{0:T(1024)S(1)}, bf16[3,16384]{1,0:T(4,128)(2,1)S(1)}, s32[]{:T(128)}, /*index=5*/s32[]{:T(128)}, s32[]{:T(128)}, s32[]{:T(128)}) while((s32[]{:T(128)}, f32[144,384]{1,0:T(8,128)S(1)}, s32[16384]{0:T(1024)S(1)}, bf16[3,16384]{1,0:T(4,128)(2,1)S(1)}, ...), condition=%wide.region_1.2_spmd.clone, body=%wide.region_0.1_spmd.clone.sunk | while | flops 230619136 | bytes 2023577 | solution.py:53
  35.3 25.7 %while.113 = (s32[]{:T(128)}, f32[144,384]{1,0:T(8,128)S(1)}, s32[32768]{0:T(1024)S(1)}, bf16[3,32768]{1,0:T(4,128)(2,1)S(1)}, s32[]{:T(128)}, /*index=5*/s32[]{:T(128)}, s32[]{:T(128)}, s32[]{:T(128)}) while((s32[]{:T(128)}, f32[144,384]{1,0:T(8,128)S(1)}, s32[32768]{0:T(1024)S(1)}, bf16[3,32768]{1,0:T(4,128)(2,1)S(1)}, ...), condition=%wide.region_3.4_spmd.clone, body=%wide.region_2.3_spmd.clone.sunk | while | flops 230619136 | bytes 2023577 | solution.py:53
  62.0 5.2 %collective-permute-start.2 = (f32[1,12,128]{2,0,1:T(1,128)S(1)}, f32[1,12,128]{2,0,1:T(1,128)S(1)}, u32[]{:S(2)}, u32[]{:S(2)}) collective-permute-start(f32[1,12,128]{2,0,1:T(1,128)S(1)} %get-tuple-element.1306), channel_id=1, source_target_pairs={{0,8},{8,16},{16,24},{24,32},{32,40},{40,48},{48,56},{56,64},{64,7... | collective-permute-start | bytes 18440 | tf_op jit(solution)/shard_map/ppermute | solution.py:22
  67.3 1.9 %collective-permute-start.4 = (f32[1,12,128]{2,0,1:T(1,128)S(1)}, f32[1,12,128]{2,0,1:T(1,128)S(1)}, u32[]{:S(2)}, u32[]{:S(2)}) collective-permute-start(f32[1,12,128]{2,0,1:T(1,128)S(1)} %get-tuple-element.1307), channel_id=1, source_target_pairs={{8,0},{16,8},{24,16},{32,24},{40,32},{48,40},{56,48},{64,56},{72,6... | collective-permute-start | bytes 18440 | tf_op jit(solution)/shard_map/ppermute | solution.py:25
  69.3 6.8 %collective-permute-done.4 = f32[1,12,128]{2,0,1:T(1,128)S(1)} collective-permute-done((f32[1,12,128]{2,0,1:T(1,128)S(1)}, f32[1,12,128]{2,0,1:T(1,128)S(1)}, u32[]{:S(2)}, u32[]{:S(2)}) %collective-permute-start.4) | collective-permute-done | bytes 6176 | tf_op jit(solution)/shard_map/ppermute | solution.py:25
  79.1 3.1 %collective-permute-done.7 = f32[14,1,128]{2,1,0:T(1,128)S(1)} collective-permute-done((f32[14,1,128]{2,1,0:T(1,128)S(1)}, f32[14,1,128]{2,1,0:T(1,128)S(1)}, u32[]{:S(2)}, u32[]{:S(2)}) %collective-permute-start.7) | collective-permute-done | bytes 7200 | tf_op jit(solution)/shard_map/ppermute | solution.py:25
  86.7 7.2 %reduce.2 = f32[1536,10]{1,0:T(8,128)S(1)} reduce(f32[1536,1,10]{2,1,0:T(1,128)S(1)} %bitcast.727, f32[]{:T(128)} %broadcast.4461), dimensions={1}, to_apply=%bitcast.559.reduce_sub_computation | reduce | bytes 122884
  95.2 6.0 %all-to-all-start = ((f32[8,1,1920]{2,1,0:T(1,128)}), f32[8,1,1920]{2,1,0:T(1,128)S(1)}, u32[]{:S(2)}, u32[]{:S(2)}) async-start(f32[8,1,1920]{2,1,0:T(1,128)} %reshape.6113), calls=%async_computation | async-start | bytes 122880 | tf_op jit(solution)/shard_map/all_to_all | solution.py:131
  101.7 5.1 %all-to-all-done = f32[8,1,1920]{2,1,0:T(1,128)S(1)} async-done(((f32[8,1,1920]{2,1,0:T(1,128)}), f32[8,1,1920]{2,1,0:T(1,128)S(1)}, u32[]{:S(2)}, u32[]{:S(2)}) %all-to-all-start) | async-done | bytes 61472 | tf_op jit(solution)/shard_map/all_to_all | solution.py:131
  112.2 3.4 %all-to-all-start.1 = ((f32[8,6,192]{2,1,0:T(8,128)}), f32[8,6,192]{2,1,0:T(8,128)S(1)}, u32[]{:S(2)}, u32[]{:S(2)}) async-start(f32[8,6,192]{2,1,0:T(8,128)} %select_maximum_fusion.1), calls=%async_computation.1 | async-start | bytes 131072 | tf_op jit(solution)/shard_map/all_to_all | solution.py:133
  115.9 5.2 %all-to-all-done.1 = f32[8,6,192]{2,1,0:T(8,128)S(1)} async-done(((f32[8,6,192]{2,1,0:T(8,128)}), f32[8,6,192]{2,1,0:T(8,128)S(1)}, u32[]{:S(2)}, u32[]{:S(2)}) %all-to-all-start.1) | async-done | bytes 36896 | tf_op jit(solution)/shard_map/all_to_all | solution.py:133
  121.4 1.9 %collective-permute-start.8 = (f32[3,1,12,128]{3,2,1,0:T(8,128)S(1)}, f32[3,1,12,128]{3,2,1,0:T(8,128)S(1)}, u32[]{:S(2)}, u32[]{:S(2)}) collective-permute-start(f32[3,1,12,128]{3,2,1,0:T(8,128)S(1)} %get-tuple-element.1281), channel_id=1, source_target_pairs={{0,8},{8,16},{16,24},{24,32},{32,40},{40,48},{48,56},{56,64},{64,7... | collective-permute-start | bytes 55304 | tf_op jit(solution)/shard_map/ppermute | solution.py:22
  123.3 4.1 %collective-permute-start.9 = (f32[3,1,12,128]{3,2,1,0:T(8,128)S(1)}, f32[3,1,12,128]{3,2,1,0:T(8,128)S(1)}, u32[]{:S(2)}, u32[]{:S(2)}) collective-permute-start(f32[3,1,12,128]{3,2,1,0:T(8,128)S(1)} %get-tuple-element.1282), channel_id=1, source_target_pairs={{8,0},{16,8},{24,16},{32,24},{40,32},{48,40},{56,48},{64,56},{72,6... | collective-permute-start | bytes 55304 | tf_op jit(solution)/shard_map/ppermute | solution.py:25
  128.3 4.1 %collective-permute-done.9 = f32[3,1,12,128]{3,2,1,0:T(8,128)S(1)} collective-permute-done((f32[3,1,12,128]{3,2,1,0:T(8,128)S(1)}, f32[3,1,12,128]{3,2,1,0:T(8,128)S(1)}, u32[]{:S(2)}, u32[]{:S(2)}) %collective-permute-start.9) | collective-permute-done | bytes 18464 | tf_op jit(solution)/shard_map/ppermute | solution.py:25
  133.7 7.2 %reduce.4 = f32[1536,10]{1,0:T(8,128)S(1)} reduce(f32[1536,1,10]{2,1,0:T(1,128)S(1)} %bitcast.729, f32[]{:T(128)} %broadcast.4461), dimensions={1}, to_apply=%bitcast.561.reduce_sub_computation | reduce | bytes 122884
  142.0 3.4 %all-to-all-start.2 = ((f32[8,1,1920]{2,1,0:T(1,128)}), f32[8,1,1920]{2,1,0:T(1,128)S(1)}, u32[]{:S(2)}, u32[]{:S(2)}) async-start(f32[8,1,1920]{2,1,0:T(1,128)} %reshape.6115), calls=%async_computation.2 | async-start | bytes 122880 | tf_op jit(solution)/shard_map/all_to_all | solution.py:131
  145.7 5.2 %all-to-all-done.2 = f32[8,1,1920]{2,1,0:T(1,128)S(1)} async-done(((f32[8,1,1920]{2,1,0:T(1,128)}), f32[8,1,1920]{2,1,0:T(1,128)S(1)}, u32[]{:S(2)}, u32[]{:S(2)}) %all-to-all-start.2) | async-done | bytes 61472 | tf_op jit(solution)/shard_map/all_to_all | solution.py:131
  156.4 3.4 %all-to-all-start.3 = ((f32[8,6,192]{2,1,0:T(8,128)}), f32[8,6,192]{2,1,0:T(8,128)S(1)}, u32[]{:S(2)}, u32[]{:S(2)}) async-start(f32[8,6,192]{2,1,0:T(8,128)} %select_maximum_fusion), calls=%async_computation.3 | async-start | bytes 131072 | tf_op jit(solution)/shard_map/all_to_all | solution.py:133
  160.3 5.0 %all-to-all-done.3 = f32[8,6,192]{2,1,0:T(8,128)S(1)} async-done(((f32[8,6,192]{2,1,0:T(8,128)}), f32[8,6,192]{2,1,0:T(8,128)S(1)}, u32[]{:S(2)}, u32[]{:S(2)}) %all-to-all-start.3) | async-done | bytes 36896 | tf_op jit(solution)/shard_map/all_to_all | solution.py:133
  (458 shorter events, 69.5 us)
Async XLA Ops:
  6.6 9.5 %copy-start.1 = (f32[3,12,12,128]{3,2,1,0:T(8,128)S(1)}, f32[3,12,12,128]{3,2,1,0:T(8,128)}, u32[]{:S(2)}) copy-start(f32[3,12,12,128]{3,2,1,0:T(8,128)} %param.22) | copy-start | bytes 663556
  6.6 15.4 %slice-start.1 = ((s32[1,1,49152]{2,1,0:T(1,128)}), s32[1,1,16384]{2,1,0:T(1,128)S(1)}, s32[]{:S(2)}) async-start(s32[1,1,49152]{2,1,0:T(1,128)} %param.19), calls=%async_computation.5 | async-start | bytes 131072 | tf_op jit(solution)/shard_map/slice | solution.py:156
  6.8 28.0 %collective-permute-start.1 = (f32[4,16384]{1,0:T(4,128)S(1)}, f32[4,16384]{1,0:T(4,128)S(1)}, u32[]{:S(2)}, u32[]{:S(2)}) collective-permute-start(f32[4,16384]{1,0:T(4,128)S(1)} %get-tuple-element.1278), channel_id=1, source_target_pairs={{8,0},{16,8},{24,16},{32,24},{40,32},{48,40},{56,48},{64,56},{72,6... | collective-permute-start | bytes 786440 | tf_op jit(solution)/shard_map/ppermute | solution.py:25
  10.1 24.8 %collective-permute-start = (f32[4,16384]{1,0:T(4,128)S(1)}, f32[4,16384]{1,0:T(4,128)S(1)}, u32[]{:S(2)}, u32[]{:S(2)}) collective-permute-start(f32[4,16384]{1,0:T(4,128)S(1)} %get-tuple-element.1277), channel_id=1, source_target_pairs={{0,8},{8,16},{16,24},{24,32},{32,40},{40,48},{48,56},{56,64},{64,7... | collective-permute-start | bytes 786440 | tf_op jit(solution)/shard_map/ppermute | solution.py:22
  16.0 67.0 %collective-permute-start.3 = (f32[3,1,12,128]{3,2,1,0:T(8,128)S(1)}, f32[3,1,12,128]{3,2,1,0:T(8,128)S(1)}, u32[]{:S(2)}, u32[]{:S(2)}) collective-permute-start(f32[3,1,12,128]{3,2,1,0:T(8,128)S(1)} %get-tuple-element.1283), channel_id=1, source_target_pairs={{0,8},{8,16},{16,24},{24,32},{32,40},{40,48},{48,56},{56,64},{64,7... | collective-permute-start | bytes 55304 | tf_op jit(solution)/shard_map/ppermute | solution.py:22
  18.0 65.1 %collective-permute-start.5 = (f32[3,1,12,128]{3,2,1,0:T(8,128)S(1)}, f32[3,1,12,128]{3,2,1,0:T(8,128)S(1)}, u32[]{:S(2)}, u32[]{:S(2)}) collective-permute-start(f32[3,1,12,128]{3,2,1,0:T(8,128)S(1)} %get-tuple-element.1284), channel_id=1, source_target_pairs={{8,0},{16,8},{24,16},{32,24},{40,32},{48,40},{56,48},{64,56},{72,6... | collective-permute-start | bytes 55304 | tf_op jit(solution)/shard_map/ppermute | solution.py:25
  61.1 8.1 %copy-start.2 = (f32[3,12,12,128]{3,2,1,0:T(8,128)S(1)}, f32[3,12,12,128]{3,2,1,0:T(8,128)}, u32[]{:S(2)}) copy-start(f32[3,12,12,128]{3,2,1,0:T(8,128)} %param.23) | copy-start | bytes 663556
  61.2 17.7 %slice-start = ((f32[3,12,12,128]{3,2,1,0:T(8,128)}), f32[1,12,12,128]{3,2,1,0:T(8,128)S(1)}, s32[]{:S(2)}) async-start(f32[3,12,12,128]{3,2,1,0:T(8,128)} %param.23), calls=%async_computation.4 | async-start | bytes 196608 | tf_op jit(solution)/shard_map/slice | solution.py:198
  62.0 7.3 %collective-permute-start.2 = (f32[1,12,128]{2,0,1:T(1,128)S(1)}, f32[1,12,128]{2,0,1:T(1,128)S(1)}, u32[]{:S(2)}, u32[]{:S(2)}) collective-permute-start(f32[1,12,128]{2,0,1:T(1,128)S(1)} %get-tuple-element.1306), channel_id=1, source_target_pairs={{0,8},{8,16},{16,24},{24,32},{32,40},{40,48},{48,56},{56,64},{64,7... | collective-permute-start | bytes 18440 | tf_op jit(solution)/shard_map/ppermute | solution.py:22
  67.3 8.8 %collective-permute-start.4 = (f32[1,12,128]{2,0,1:T(1,128)S(1)}, f32[1,12,128]{2,0,1:T(1,128)S(1)}, u32[]{:S(2)}, u32[]{:S(2)}) collective-permute-start(f32[1,12,128]{2,0,1:T(1,128)S(1)} %get-tuple-element.1307), channel_id=1, source_target_pairs={{8,0},{16,8},{24,16},{32,24},{40,32},{48,40},{56,48},{64,56},{72,6... | collective-permute-start | bytes 18440 | tf_op jit(solution)/shard_map/ppermute | solution.py:25
  76.1 2.9 %collective-permute-start.6 = (f32[14,1,128]{2,1,0:T(1,128)S(1)}, f32[14,1,128]{2,1,0:T(1,128)S(1)}, u32[]{:S(2)}, u32[]{:S(2)}) collective-permute-start(f32[14,1,128]{2,1,0:T(1,128)S(1)} %get-tuple-element.1290), channel_id=1, source_target_pairs={{0,1},{1,2},{2,3},{3,4},{4,5},{5,6},{6,7},{8,9},{9,10},{10,11},{11... | collective-permute-start | bytes 21512 | tf_op jit(solution)/shard_map/ppermute | solution.py:22
  77.4 4.8 %collective-permute-start.7 = (f32[14,1,128]{2,1,0:T(1,128)S(1)}, f32[14,1,128]{2,1,0:T(1,128)S(1)}, u32[]{:S(2)}, u32[]{:S(2)}) collective-permute-start(f32[14,1,128]{2,1,0:T(1,128)S(1)} %get-tuple-element.1289), channel_id=1, source_target_pairs={{1,0},{2,1},{3,2},{4,3},{5,4},{6,5},{7,6},{9,8},{10,9},{11,10},{12... | collective-permute-start | bytes 21512 | tf_op jit(solution)/shard_map/ppermute | solution.py:25
  93.9 7.5 %copy-start.5 = (f32[2,12,1,128]{3,2,1,0:T(1,128)S(1)}, f32[2,12,1,128]{3,2,1,0:T(1,128)}, u32[]{:S(2)}) copy-start(f32[2,12,1,128]{3,2,1,0:T(1,128)} %get-tuple-element.1128) | copy-start | bytes 36868
  93.9 7.5 %copy-start.6 = (f32[2,12,1,128]{3,2,1,0:T(1,128)S(1)}, f32[2,12,1,128]{3,2,1,0:T(1,128)}, u32[]{:S(2)}) copy-start(f32[2,12,1,128]{3,2,1,0:T(1,128)} %get-tuple-element.1129) | copy-start | bytes 36868
  93.9 7.5 %copy-start.7 = (f32[2,12,1,128]{3,2,1,0:T(1,128)S(1)}, f32[2,12,1,128]{3,2,1,0:T(1,128)}, u32[]{:S(2)}) copy-start(f32[2,12,1,128]{3,2,1,0:T(1,128)} %get-tuple-element.1130) | copy-start | bytes 36868
  93.9 7.5 %copy-start.8 = (f32[2,12,1,128]{3,2,1,0:T(1,128)S(1)}, f32[2,12,1,128]{3,2,1,0:T(1,128)}, u32[]{:S(2)}) copy-start(f32[2,12,1,128]{3,2,1,0:T(1,128)} %get-tuple-element.1131) | copy-start | bytes 36868
  93.9 7.5 %copy-start.9 = (f32[2,12,1,128]{3,2,1,0:T(1,128)S(1)}, f32[2,12,1,128]{3,2,1,0:T(1,128)}, u32[]{:S(2)}) copy-start(f32[2,12,1,128]{3,2,1,0:T(1,128)} %get-tuple-element.1132) | copy-start | bytes 36868
  93.9 7.5 %copy-start.10 = (f32[2,12,1,128]{3,2,1,0:T(1,128)S(1)}, f32[2,12,1,128]{3,2,1,0:T(1,128)}, u32[]{:S(2)}) copy-start(f32[2,12,1,128]{3,2,1,0:T(1,128)} %get-tuple-element.1133) | copy-start | bytes 36868
  95.2 11.6 %all-to-all-start = ((f32[8,1,1920]{2,1,0:T(1,128)}), f32[8,1,1920]{2,1,0:T(1,128)S(1)}, u32[]{:S(2)}, u32[]{:S(2)}) async-start(f32[8,1,1920]{2,1,0:T(1,128)} %reshape.6113), calls=%async_computation | async-start | bytes 122880 | tf_op jit(solution)/shard_map/all_to_all | solution.py:131
  112.2 8.9 %all-to-all-start.1 = ((f32[8,6,192]{2,1,0:T(8,128)}), f32[8,6,192]{2,1,0:T(8,128)S(1)}, u32[]{:S(2)}, u32[]{:S(2)}) async-start(f32[8,6,192]{2,1,0:T(8,128)} %select_maximum_fusion.1), calls=%async_computation.1 | async-start | bytes 131072 | tf_op jit(solution)/shard_map/all_to_all | solution.py:133
  121.4 6.9 %collective-permute-start.8 = (f32[3,1,12,128]{3,2,1,0:T(8,128)S(1)}, f32[3,1,12,128]{3,2,1,0:T(8,128)S(1)}, u32[]{:S(2)}, u32[]{:S(2)}) collective-permute-start(f32[3,1,12,128]{3,2,1,0:T(8,128)S(1)} %get-tuple-element.1281), channel_id=1, source_target_pairs={{0,8},{8,16},{16,24},{24,32},{32,40},{40,48},{48,56},{56,64},{64,7... | collective-permute-start | bytes 55304 | tf_op jit(solution)/shard_map/ppermute | solution.py:22
  123.3 9.0 %collective-permute-start.9 = (f32[3,1,12,128]{3,2,1,0:T(8,128)S(1)}, f32[3,1,12,128]{3,2,1,0:T(8,128)S(1)}, u32[]{:S(2)}, u32[]{:S(2)}) collective-permute-start(f32[3,1,12,128]{3,2,1,0:T(8,128)S(1)} %get-tuple-element.1282), channel_id=1, source_target_pairs={{8,0},{16,8},{24,16},{32,24},{40,32},{48,40},{56,48},{64,56},{72,6... | collective-permute-start | bytes 55304 | tf_op jit(solution)/shard_map/ppermute | solution.py:25
  142.0 8.9 %all-to-all-start.2 = ((f32[8,1,1920]{2,1,0:T(1,128)}), f32[8,1,1920]{2,1,0:T(1,128)S(1)}, u32[]{:S(2)}, u32[]{:S(2)}) async-start(f32[8,1,1920]{2,1,0:T(1,128)} %reshape.6115), calls=%async_computation.2 | async-start | bytes 122880 | tf_op jit(solution)/shard_map/all_to_all | solution.py:131
  156.4 8.9 %all-to-all-start.3 = ((f32[8,6,192]{2,1,0:T(8,128)}), f32[8,6,192]{2,1,0:T(8,128)S(1)}, u32[]{:S(2)}, u32[]{:S(2)}) async-start(f32[8,6,192]{2,1,0:T(8,128)} %select_maximum_fusion), calls=%async_computation.3 | async-start | bytes 131072 | tf_op jit(solution)/shard_map/all_to_all | solution.py:133
  (7 other events, 39.3 us)
where the time goes:
time: 167 us; the launch traced here: 166 us
  starting transfers between devices  47 us (28%)
  other arithmetic  40.1 us (24%)
  waiting for transfers between devices  34.5 us (21%)
  matrix products  26.3 us (16%)
  local copies, waits for them, and re-layouts  13.4 us (8%)
  loops' own time  3 us (2%)
  between operations  1.84 us (1%)
    dot_general x24, matrix products, accumulate(): lax.dot_general(plane_hot, spread, (((0,), (1,)), ((), ())), preferred_el...  26.3 us
    ppermute x5, starting transfers between devices, extended(): lax.ppermute(lax.slice_in_dim(block, block.shape[dim] - width, None, axis...  16.3 us
    ppermute x5, starting transfers between devices, extended(): lax.ppermute(lax.slice_in_dim(block, 0, width, axis=dim), axis, backward)  14.7 us
    unnamed x10, other arithmetic  14.3 us
    ppermute x5, waiting for transfers between devices, extended(): lax.ppermute(lax.slice_in_dim(block, 0, width, axis=dim), axis, backward)  14 us
    all_to_all x2, waiting for transfers between devices, reduced_boundary(): lax.all_to_all(interface, 'rad', split_axis=2, concat_axis=0, tiled=True)  10.3 us
    all_to_all x2, waiting for transfers between devices, reduced_boundary(): lax.all_to_all(solved, 'rad', split_axis=0, concat_axis=2, tiled=True)[0]  10.1 us
    all_to_all x2, starting transfers between devices, reduced_boundary(): lax.all_to_all(interface, 'rad', split_axis=2, concat_axis=0, tiled=True)  9.36 us
  transfers between devices with their start and end apart: 14, of which 7 were waited for; matrix products, arithmetic and copies ran while one was open for 25% of the time, Pallas kernels for 0%

commit v1 on v0

v1 whole, which is shorter than its diff:
```python
import functools

import jax
import jax.numpy as jnp
from jax import lax
from jax.experimental import pallas as pl
from jax.experimental.pallas import tpu as pltpu
from jax.sharding import PartitionSpec as P

MESH = pl.DeviceIdType.MESH
F32 = jnp.float32
BF16 = jnp.bfloat16

SWEEPS = 2
LATERAL = 0.015625
RADIAL = 32.0
BUOYANCY = 0.1
PRIOR_WEIGHT = 0.5
CONTRAST_BASALT = 2.3
CONTRAST_MELT = 1.5

SLOTS = 16
HALO = 2
LANES = 128
Q1 = 24
Q2 = 16


def side_index(cell, first_plane, cr):
    rows = (cell >> 7) - first_plane * cr
    plane = (rows >= cr).astype(jnp.int32)
    radial = rows - cr * plane
    return (plane * 2 + (radial & 1)) * 8 + (radial >> 1)


def stay_index(cell, cr):
    rows = cell >> 8
    half = cr // 2
    plane = (rows * 43691) >> 18
    return (rows - half * plane) * SLOTS + plane + HALO


def hot_masks(index, tiles):
    base = lax.broadcasted_iota(jnp.int32, (16, LANES), 0).astype(F32)
    return [index == (base + 16.0 * t).astype(BF16) for t in range(tiles)]


def bin_group(acc, loads, index_a, index_b, first_row, rows, step_rows, tiles_a, tiles_b, total_rows):
    zero = jnp.zeros((16, LANES), BF16)
    one = jnp.ones((16, LANES), BF16)

    def spread(ref, row):
        return jnp.broadcast_to(ref[pl.ds(row, 1), :], (16, LANES)).astype(BF16)

    def body(step, carry):
        left, right = [], []
        for j in range(step_rows):
            row = first_row + step * step_rows + j
            values = [spread(loads, q * total_rows + row) for q in range(3)]
            hot_a = hot_masks(spread(index_a, row), tiles_a)
            hot_b = hot_masks(spread(index_b, row), tiles_b)
            left.append(jnp.concatenate([jnp.where(h, v, zero) for v in values for h in hot_a], 0))
            right.append(jnp.concatenate([jnp.where(h, one, zero) for h in hot_b], 0))
        acc[...] += lax.dot_general(
            jnp.concatenate(left, 1),
            jnp.concatenate(right, 1),
            (((1,), (1,)), ((), ())),
            preferred_element_type=F32,
        )
        return carry

    lax.fori_loop(0, rows // step_rows, body, 0)


def kernel(
    nl, nk, vals, cell, cnt, bv, vel, frc, out, comp,
    loads, index_a, index_b, acc_s, acc_0, acc_2, edge_lo, edge_hi, got_a_lo, got_a_hi, got_b_lo, got_b_hi,
    hv_lo, hv_hi, hf_lo, hf_hi, hb_lo, hb_hi,
    ext, vs, fs, bs, visc, f_w, f_e, f_s, f_n, up, ip, res0, res1, part,
    snd1, rcv1, bck1, ans1, snd2, rcv2, bck2, ans2,
    lat_send, lat_recv, rad_send, rad_recv,
):
    cx, cr = bv.shape[0], bv.shape[1]
    total_rows = cell.shape[0]
    rows = total_rows // 3
    l = lax.axis_index("lat")
    k = lax.axis_index("rad")
    lm = lax.rem(l + nl - 1, nl)
    lp = lax.rem(l + 1, nl)
    first_l, last_l = l == 0, l == nl - 1

    barrier = pltpu.get_barrier_semaphore()
    for other in (lm, lp):
        pl.semaphore_signal(barrier, inc=1, device_id=(other, k), device_id_type=MESH)
    for d in range(1, nk):
        pl.semaphore_signal(barrier, inc=1, device_id=(l, lax.rem(k + d, nk)), device_id_type=MESH)

    def to_lat(src, dst, other, n):
        return pltpu.make_async_remote_copy(
            src_ref=src, dst_ref=dst, send_sem=lat_send.at[n], recv_sem=lat_recv.at[n],
            device_id=(other, k), device_id_type=MESH,
        )

    place = lax.broadcasted_iota(jnp.int32, (rows, LANES), 0) * LANES + lax.broadcasted_iota(
        jnp.int32, (rows, LANES), 1
    )
    for g in (0, 2, 1):
        sl = pl.ds(g * rows, rows)
        weight = jnp.where(place < cnt[0, 0, g], 0.5 + vals[sl, :], 0.0)
        loads[sl, :] = weight
        loads[pl.ds(total_rows + g * rows, rows), :] = weight * vals[pl.ds(total_rows + g * rows, rows), :]
        loads[pl.ds(2 * total_rows + g * rows, rows), :] = weight * vals[pl.ds(2 * total_rows + g * rows, rows), :]
        c = cell[sl, :]
        if g == 1:
            index_a[sl, :] = stay_index(c, cr).astype(F32)
            index_b[sl, :] = (c & 255).astype(F32)
        else:
            index_a[sl, :] = side_index(c, cx - HALO if g == 0 else 0, cr).astype(F32)
            index_b[sl, :] = (c & 127).astype(F32)

    step_rows = min(32, rows)
    acc_0[...] = jnp.zeros_like(acc_0)
    acc_2[...] = jnp.zeros_like(acc_2)
    acc_s[...] = jnp.zeros_like(acc_s)
    bin_group(acc_0, loads, index_a, index_b, 0, rows, step_rows, 2, 8, total_rows)
    bin_group(acc_2, loads, index_a, index_b, 2 * rows, rows, step_rows, 2, 8, total_rows)

    pl.semaphore_wait(barrier, nk + 1)
    early = [
        to_lat(acc_0, got_a_hi, lm, 0),
        to_lat(acc_2, got_a_lo, lp, 1),
        to_lat(vel.at[:, pl.ds(0, HALO)], hv_hi, lm, 2),
        to_lat(vel.at[:, pl.ds(cx - HALO, HALO)], hv_lo, lp, 3),
        to_lat(frc.at[:, pl.ds(0, 1)], hf_hi, lm, 4),
        to_lat(frc.at[:, pl.ds(cx - 1, 1)], hf_lo, lp, 5),
        to_lat(bv.at[pl.ds(0, HALO)], hb_hi, lm, 6),
        to_lat(bv.at[pl.ds(cx - HALO, HALO)], hb_lo, lp, 7),
    ]
    for copy in early:
        copy.start()

    bin_group(acc_s, loads, index_a, index_b, rows, rows, step_rows, 6, 16, total_rows)

    half = cr // 2
    for q in range(3):
        for h in range(2):
            for s in range(HALO):
                row = q * 32 + (s * 2 + h) * 8
                lanes = pl.ds(h * LANES, LANES)
                edge_lo[pl.ds(row, 8), :] = jnp.zeros((8, LANES), F32)
                edge_hi[pl.ds(row, 8), :] = jnp.zeros((8, LANES), F32)
                for p in range(half):
                    base = q * half * SLOTS + p * SLOTS
                    edge_lo[pl.ds(row + p, 1), :] = acc_s[pl.ds(base + HALO + s, 1), lanes]
                    edge_hi[pl.ds(row + p, 1), :] = acc_s[pl.ds(base + HALO + cx - HALO + s, 1), lanes]
    late = [to_lat(edge_lo, got_b_hi, lm, 8), to_lat(edge_hi, got_b_lo, lp, 9)]
    for copy in late:
        copy.start()

    def put(dst, base, slot, value):
        dst[pl.ds(base + slot, cr, stride=SLOTS), :] = value

    keep_lo = jnp.where(first_l, 0.0, 1.0)
    keep_hi = jnp.where(last_l, 0.0, 1.0)
    zeros = jnp.zeros((cr, LANES), F32)
    for x in range(cx):
        put(bs, 0, x + HALO, bv[x])
        for c in range(3):
            put(vs, c * cr * SLOTS, x + HALO, vel[c, x])
            put(fs, c * cr * SLOTS, x + HALO, frc[c, x])
    for c in range(3):
        put(fs, c * cr * SLOTS, 0, zeros)
        put(fs, c * cr * SLOTS, SLOTS - 1, zeros)
    ext[...] = jnp.zeros_like(ext)
    for copy in early[2:]:
        copy.wait_recv()
    for s in range(HALO):
        put(bs, 0, s, hb_lo[s])
        put(bs, 0, SLOTS - HALO + s, hb_hi[s])
        for c in range(3):
            put(vs, c * cr * SLOTS, s, hv_lo[c, s] * keep_lo)
            put(vs, c * cr * SLOTS, SLOTS - HALO + s, hv_hi[c, s] * keep_hi)
    for c in range(3):
        put(fs, c * cr * SLOTS, HALO - 1, hf_lo[c, 0])
        put(fs, c * cr * SLOTS, SLOTS - HALO, hf_hi[c, 0])

    def put_edge(ref, slot, scale):
        for q in range(3):
            for h in range(2):
                for s in range(HALO):
                    value = ref[pl.ds(q * 32 + (s * 2 + h) * 8, half), :] * scale
                    ext[pl.ds(q * cr * SLOTS + h * SLOTS + slot + s, half, stride=2 * SLOTS), :] = value

    early[0].wait_recv()
    early[1].wait_recv()
    put_edge(got_a_lo, HALO, keep_lo)
    put_edge(got_a_hi, SLOTS - 2 * HALO, keep_hi)
    for copy in late:
        copy.wait_recv()
    got_b_lo[...] += acc_0[...]
    got_b_hi[...] += acc_2[...]
    put_edge(got_b_lo, 0, 1.0)
    put_edge(got_b_hi, SLOTS - HALO, 1.0)

    slot = lax.broadcasted_iota(jnp.int32, (SLOTS, LANES), 0)
    lane = lax.broadcasted_iota(jnp.int32, (SLOTS, LANES), 1)
    low = jnp.where(first_l, HALO, 0)
    high = jnp.where(last_l, SLOTS - HALO, SLOTS)
    inside = jnp.where((slot >= low) & (slot < high), 1.0, 0.0)
    is_west = lane == 0
    is_east = lane == LANES - 1

    def at(r, c=0):
        return pl.ds((c * cr + r) * SLOTS, SLOTS)

    def west(v):
        return pltpu.roll(v, 1, 0)

    def east(v):
        return pltpu.roll(v, SLOTS - 1, 0)

    def south(v):
        return jnp.where(is_west, 0.0, pltpu.roll(v, 1, 1))

    def north(v):
        return jnp.where(is_east, 0.0, pltpu.roll(v, LANES - 1, 1))

    for r in range(cr):
        lanes = pl.ds((r & 1) * LANES, LANES)
        sums = [acc_s[pl.ds((q * half + r // 2) * SLOTS, SLOTS), lanes] + ext[at(r, q), :] for q in range(3)]
        inverse = 1.0 / (sums[0] + PRIOR_WEIGHT)
        basalt = sums[1] * inverse
        melt = sums[2] * inverse
        comp[0, r] = basalt
        comp[1, r] = melt
        fs[at(r, 2), :] = fs[at(r, 2), :] - BUOYANCY * basalt
        visc[at(r), :] = inside * (bs[at(r), :] * jnp.exp(CONTRAST_BASALT * basalt - CONTRAST_MELT * melt))

    weight_lo = jnp.where(k == 0, 0.5 * RADIAL, RADIAL)
    weight_hi = jnp.where(k == nk - 1, 0.5 * RADIAL, RADIAL)

    def below(r):
        if r == 0:
            return weight_lo * visc[at(0), :]
        return 0.5 * RADIAL * (visc[at(r - 1), :] + visc[at(r), :])

    def above(r):
        if r == cr - 1:
            return weight_hi * visc[at(cr - 1), :]
        return below(r + 1)

    forward = None
    for r in range(cr):
        v = visc[at(r), :]
        scale = LATERAL * 0.5
        fw, fe, fs_, fn = (scale * (v + side(v)) for side in (west, east, south, north))
        f_w[at(r), :] = fw
        f_e[at(r), :] = fe
        f_s[at(r), :] = fs_
        f_n[at(r), :] = fn
        diagonal = fw + fe + fs_ + fn + below(r) + above(r)
        diagonal = jnp.where(v > 0.0, diagonal, 1.0)
        if r > 0:
            diagonal = diagonal - below(r) * up[at(r - 1), :]
        inverse = 1.0 / diagonal
        ip[at(r), :] = inverse
        if r < cr - 1:
            up[at(r), :] = above(r) * inverse
        forward = inverse if r == 0 else below(r) * forward * inverse
        res0[at(r), :] = forward
    backward = ip[at(cr - 1), :]
    backward0 = res0[at(cr - 1), :]
    res1[at(cr - 1), :] = backward
    for r in range(cr - 2, -1, -1):
        u = up[at(r), :]
        backward = u * backward
        res1[at(r), :] = backward
        backward0 = res0[at(r), :] + u * backward0
        res0[at(r), :] = backward0

    def particular(current):
        for c in range(3):
            carried = None
            for r in range(cr):
                v = current[at(r, c), :]
                right = (
                    fs[at(r, c), :]
                    + f_w[at(r), :] * west(v)
                    + f_e[at(r), :] * east(v)
                    + f_s[at(r), :] * south(v)
                    + f_n[at(r), :] * north(v)
                )
                carried = right if r == 0 else right + below(r) * carried
                carried = carried * ip[at(r), :]
                part[at(r, c), :] = carried
            for r in range(cr - 2, -1, -1):
                carried = part[at(r, c), :] + up[at(r), :] * carried
                part[at(r, c), :] = carried

    def exchange(src, dst, size, phase):
        copies = []
        for d in range(1, nk):
            other = lax.rem(k + d, nk)
            n = phase * (nk - 1) + d - 1
            copies.append(
                pltpu.make_async_remote_copy(
                    src_ref=src.at[pl.ds(pl.multiple_of(other * size, 8), size)],
                    dst_ref=dst.at[pl.ds(pl.multiple_of(k * size, 8), size)],
                    send_sem=rad_send.at[n], recv_sem=rad_recv.at[n],
                    device_id=(l, other), device_id_type=MESH,
                )
            )
        for copy in copies:
            copy.start()
        mine = pl.ds(pl.multiple_of(k * size, 8), size)
        dst[mine, :] = src[mine, :]
        return copies

    def to_solvers(dst, size, number, value):
        for t in range(2):
            dst[pl.ds(number * 2 + t, nk, stride=size), :] = value[t * 8:(t + 1) * 8]

    def from_solvers(src, number):
        return jnp.concatenate([src[pl.ds(number * 2 + t, nk, stride=Q2), :] for t in range(2)], 0)

    def piece(src, size, i, number):
        return src[pl.ds(i * size + number * 2, 2), :]

    def apply(answers, store):
        for c in range(3):
            low_flux = from_solvers(answers, c)
            high_flux = from_solvers(answers, 3 + c)
            for r in range(cr):
                value = part[at(r, c), :] + res0[at(r), :] * low_flux + res1[at(r), :] * high_flux
                store(c, r, value)

    def solve(factors, source, size, first, back):
        sums = [piece(source, size, 0, first + 3 + c) for c in range(3)]
        fixed = [[piece(source, size, 0, first + c) for c in range(3)]]
        olds = [None]
        for i in range(1, nk):
            f = factors[i]
            olds.append([s * f["ih"] for s in sums])
            fixed.append([f["cf"] * piece(source, size, i, first + c) + f["cp"] * sums[c] for c in range(3)])
            sums = [
                piece(source, size, i, first + 3 + c) + f["e1"] * sums[c] + f["e2"] * fixed[i][c] for c in range(3)
            ]
        for c in range(3):
            flux = None
            back[pl.ds((nk - 1) * Q2 + (3 + c) * 2, 2), :] = jnp.zeros((2, LANES), F32)
            back[pl.ds(c * 2, 2), :] = jnp.zeros((2, LANES), F32)
            for i in range(nk - 1, 0, -1):
                f = factors[i]
                first_value = fixed[i][c] if flux is None else fixed[i][c] + f["f1"] * flux
                last_value = olds[i][c] + f["qq"] * first_value
                back[pl.ds(i * Q2 + c * 2, 2), :] = f["fb"] * last_value + f["dl"] * first_value
                flux = f["fb"] * first_value - f["dl"] * last_value
                back[pl.ds((i - 1) * Q2 + (3 + c) * 2, 2), :] = flux

    particular(vs)
    for number, value in enumerate(
        [res0[at(0), :], res1[at(0), :], res1[at(cr - 1), :], visc[at(0), :], visc[at(cr - 1), :]]
        + [part[at(0, c), :] for c in range(3)]
        + [part[at(cr - 1, c), :] for c in range(3)]
    ):
        to_solvers(snd1, Q1, number, value)
    sent = exchange(snd1, rcv1, Q1, 0)
    for copy in sent:
        copy.wait_recv()
    everything = early + late + sent

    factors = [None]
    slope = piece(rcv1, Q1, 0, 2)
    for i in range(1, nk):
        a, b, d, v_first = (piece(rcv1, Q1, i, n) for n in (0, 1, 2, 3))
        v_last = piece(rcv1, Q1, i - 1, 4)
        fb = 0.5 * RADIAL * (v_last + v_first)
        dl = 0.5 * RADIAL * (v_first - v_last)
        afb = a * fb
        h = 1.0 + slope * dl
        inverse_h = 1.0 / h
        inverse = 1.0 / (h * (1.0 - a * dl) - afb * (fb * slope))
        qq = fb * slope * inverse_h
        cf = h * inverse
        f1 = cf * b
        e2 = b * (fb * qq + dl)
        factors.append(dict(fb=fb, dl=dl, ih=inverse_h, qq=qq, cf=cf, cp=afb * inverse, f1=f1, e1=b * fb * inverse_h, e2=e2))
        slope = d + e2 * f1
    solve(factors, rcv1, Q1, 5, bck1)
    sent = exchange(bck1, ans1, Q2, 1)
    for copy in sent:
        copy.wait_recv()
    everything += sent

    def store_current(c, r, value):
        vs[at(r, c), :] = value * inside

    apply(ans1, store_current)

    particular(vs)
    for c in range(3):
        to_solvers(snd2, Q2, c, part[at(0, c), :])
        to_solvers(snd2, Q2, 3 + c, part[at(cr - 1, c), :])
    sent = exchange(snd2, rcv2, Q2, 2)
    for copy in sent:
        copy.wait_recv()
    everything += sent
    solve(factors, rcv2, Q2, 0, bck2)
    sent = exchange(bck2, ans2, Q2, 3)
    for copy in sent:
        copy.wait_recv()
    everything += sent

    def store_out(c, r, value):
        out[c, r] = value

    apply(ans2, store_out)
    for copy in everything:
        copy.wait_send()


def solution(mesh):
    nl, nk = mesh.shape["lat"], mesh.shape["rad"]

    def local(tracer_values, tracer_cell, tracer_count, base_viscosity, velocity, forcing):
        cx, cr, ny = base_viscosity.shape
        slots = tracer_cell.shape[2]
        assert nk == 8 and cx + 2 * HALO == SLOTS and ny == LANES and cr == 12
        total_rows = slots // LANES
        vmem = functools.partial(pltpu.VMEM, dtype=F32)
        field = cr * SLOTS
        spare = 8 * SLOTS
        scratch = [
            vmem((3 * total_rows, LANES)), vmem((total_rows, LANES)), vmem((total_rows, LANES)),
            vmem((3 * field // 2, 2 * LANES)),
        ]
        scratch += [vmem((96, LANES))] * 8
        scratch += [vmem((3, HALO, cr, LANES))] * 2 + [vmem((3, 1, cr, LANES))] * 2 + [vmem((HALO, cr, LANES))] * 2
        scratch += [vmem((3 * field + 2 * spare, LANES))] + [vmem((3 * field + spare, LANES))] * 2 + [vmem((field + spare, LANES))]
        scratch += [vmem((field, LANES))] * 9 + [vmem((3 * field, LANES))]
        scratch += [vmem((nk * Q1, LANES))] * 2 + [vmem((nk * Q2, LANES))] * 6
        scratch += [pltpu.SemaphoreType.DMA((10,))] * 2 + [pltpu.SemaphoreType.DMA((4 * (nk - 1),))] * 2
        v = pl.BlockSpec(memory_space=pltpu.VMEM)
        smoothed, composition = pl.pallas_call(
            functools.partial(kernel, nl, nk),
            out_shape=[
                jax.ShapeDtypeStruct((3, cr, SLOTS, ny), F32),
                jax.ShapeDtypeStruct((2, cr, SLOTS, ny), F32),
            ],
            in_specs=[v, v, pl.BlockSpec(memory_space=pltpu.SMEM), v, v, v],
            out_specs=[v, v],
            scratch_shapes=scratch,
            compiler_params=pltpu.CompilerParams(collective_id=0, has_side_effects=True),
        )(
            tracer_values.reshape(3 * total_rows, LANES),
            tracer_cell.reshape(total_rows, LANES),
            tracer_count,
            base_viscosity,
            velocity,
            forcing,
        )
        own = slice(HALO, HALO + cx)
        return (
            jnp.transpose(smoothed[:, :, own], (0, 2, 1, 3)),
            jnp.transpose(composition[:, :, own], (0, 2, 1, 3)),
        )

    return jax.shard_map(
        local,
        mesh=mesh,
        in_specs=(
            P("lat", "rad", None, None),
            P("lat", "rad", None),
            P("lat", "rad", None),
            P("lat", "rad", None),
            P(None, "lat", "rad", None),
            P(None, "lat", "rad", None),
        ),
        out_specs=(P(None, "lat", "rad", None), P(None, "lat", "rad", None)),
        check_vma=False,
    )
```

time: 167 us -> 45.8 us (0.27)
  the two profiles are of different devices: /device:TPU:248 before, /device:TPU:1 now
where the time goes in v1:
time: 45.8 us; the launch traced here: 45.6 us
  Pallas kernels  42.2 us (92%)
  local copies, waits for them, and re-layouts  2.7 us (6%)
  between operations  0.65 us (1%)
    pallas_call x1, Pallas kernels, local(): pl.pallas_call(functools.partial(kernel, nl, nk), out_shape=[jax.ShapeDty...  42.2 us
    unnamed x4, local copies, waits for them, and re-layouts  1.7 us
    transpose x1, local copies, waits for them, and re-layouts, local(): jnp.transpose(smoothed[:, :, own], (0, 2, 1, 3))  0.99 us

profile of v1, /device:TPU:1, one launch (start us, length us, event | category | flops | bytes accessed | tf_op | source)
XLA Modules:
  0.0 45.6 jit_solution(10367040072922858586)
XLA Ops:
  0.6 42.2 %shard_map.77 = (f32[3,12,16,128]{3,2,1,0:T(8,128)}, f32[2,12,16,128]{3,2,1,0:T(8,128)}) custom-call(f32[1152,128]{1,0:T(8,128)} %bitcast.6, s32[384,128]{1,0:T(8,128)} %bitcast.7, s32[1,1,3]{2,1,0:T(1,128)} %cnt.1, f32[12,12,128]{2,1,0:T(8,128)} %bv.1, f32[3,12,12,128]{3,2,1,0:T(8,128)} %vel.1, f32[3,12,12,128]{3,2,1,0:T(8,128)} %frc.1), custom_call_target="tpu_custom_call" | custom-call | tf_op jit(solution)/shard_map/pallas_call | solution.py:444
  42.9 1.0 %slice_bitcast_fusion = f32[3,12,12,128]{3,1,2,0:T(8,128)S(1)} fusion(f32[3,12,16,128]{3,2,1,0:T(8,128)} %get-tuple-element.4), kind=kLoop, calls=%fused_computation | loop fusion | bytes 442368 | tf_op jit(solution)/shard_map/transpose | solution.py:464
  43.9 0.0 copy-start
  43.9 0.8 %copy.8 = f32[3,12,12,128]{3,2,1,0:T(8,128)} copy(f32[3,12,12,128]{3,1,2,0:T(8,128)S(1)} %slice_bitcast_fusion) | data formatting | bytes 442368
  44.6 0.1 copy-done
  44.8 0.8 %copy.9 = f32[2,12,12,128]{3,0,2,1:T(2,128)} copy(f32[2,12,12,128]{3,1,2,0:T(8,128)S(1)} %slice_bitcast_fusion.1) | data formatting | bytes 294912
  (1 shorter events, 0.0 us)
Async XLA Ops:
  43.9 0.9 %copy-start = (f32[2,12,16,128]{3,2,1,0:T(8,128)S(1)}, f32[2,12,16,128]{3,2,1,0:T(8,128)}, u32[]{:S(2)}) copy-start(f32[2,12,16,128]{3,2,1,0:T(8,128)} %get-tuple-element.5) | copy-start | bytes 589828

commit v2 on v1

v2 whole, which is shorter than its diff:
```python
import functools

import jax
import jax.numpy as jnp
from jax import lax
from jax.experimental import pallas as pl
from jax.experimental.pallas import tpu as pltpu
from jax.sharding import PartitionSpec as P

MESH = pl.DeviceIdType.MESH
F32 = jnp.float32
BF16 = jnp.bfloat16

SWEEPS = 2
LATERAL = 0.015625
RADIAL = 32.0
BUOYANCY = 0.1
PRIOR_WEIGHT = 0.5
CONTRAST_BASALT = 2.3
CONTRAST_MELT = 1.5

SLOTS = 16
HALO = 2
LANES = 128
WINDOW = 8
Q1 = 11 * WINDOW
Q2 = 6 * WINDOW


def side_index(cell, first_plane, cr):
    rows = (cell >> 7) - first_plane * cr
    plane = (rows >= cr).astype(jnp.int32)
    radial = rows - cr * plane
    return (plane * 2 + (radial & 1)) * 8 + (radial >> 1)


def stay_index(cell, cr):
    rows = cell >> 8
    half = cr // 2
    plane = (rows * 43691) >> 18
    return (rows - half * plane) * SLOTS + plane + HALO


def hot_masks(index, tiles):
    base = lax.broadcasted_iota(jnp.int32, (16, LANES), 0).astype(F32)
    return [index == (base + 16.0 * t).astype(BF16) for t in range(tiles)]


def bin_group(acc, loads, index_a, index_b, first_row, rows, step_rows, tiles_a, tiles_b, total_rows):
    zero = jnp.zeros((16, LANES), BF16)
    one = jnp.ones((16, LANES), BF16)

    def spread(ref, row):
        return jnp.broadcast_to(ref[pl.ds(row, 1), :], (16, LANES)).astype(BF16)

    def body(step, carry):
        left, right = [], []
        for j in range(step_rows):
            row = first_row + step * step_rows + j
            values = [spread(loads, q * total_rows + row) for q in range(3)]
            hot_a = hot_masks(spread(index_a, row), tiles_a)
            hot_b = hot_masks(spread(index_b, row), tiles_b)
            left.append(jnp.concatenate([jnp.where(h, v, zero) for v in values for h in hot_a], 0))
            right.append(jnp.concatenate([jnp.where(h, one, zero) for h in hot_b], 0))
        acc[...] += lax.dot_general(
            jnp.concatenate(left, 1),
            jnp.concatenate(right, 1),
            (((1,), (1,)), ((), ())),
            preferred_element_type=F32,
        )
        return carry

    lax.fori_loop(0, rows // step_rows, body, 0)


def kernel(
    nl, nk, vals, cell, cnt, bv, vel, frc, out, comp,
    loads, index_a, index_b, acc_s, acc_side, edge_lo, edge_hi, got_a, got_b, got_c, got_s,
    hv, hf, hb, pv, pf, pb,
    ext, vs, fs, bs, visc, f_w, f_e, f_s, f_n, up, ip, res0, res1, part, mix,
    snd1, rcv1, snd2, rcv2, flux_lo, flux_hi, share, fin, ret,
    lat_send, lat_recv, chip_send, chip_recv, rad_send, rad_recv,
):
    cx, cr = bv.shape[0], bv.shape[1]
    rows_all = 2 * cr
    half = cr // 2
    total_rows = cell.shape[0]
    rows = total_rows // 3
    nc = nk // 2
    l = lax.axis_index("lat")
    k = lax.axis_index("rad")
    kc = k // 2
    par = lax.rem(k, 2)
    lm = lax.rem(l + nl - 1, nl)
    lp = lax.rem(l + 1, nl)
    odd_below = (lm, 2 * kc + 1)
    even_above = (lp, 2 * kc)
    partner = (l, 2 * kc + 1 - par)
    peers = [(l, 2 * lax.rem(kc + d, nc) + par) for d in range(1, nc)]
    window = par * 6

    barrier = pltpu.get_barrier_semaphore()
    beside = lm + par * (lp - lm)
    for device in [(beside, 2 * kc), (beside, 2 * kc + 1), partner] + peers:
        pl.semaphore_signal(barrier, inc=1, device_id=device, device_id_type=MESH)

    def remote(src, dst, device, send, recv):
        return pltpu.make_async_remote_copy(
            src_ref=src, dst_ref=dst, send_sem=send, recv_sem=recv, device_id=device, device_id_type=MESH
        )

    def to_lat(low, high, dst, n):
        return [
            remote(low, dst.at[par], odd_below, lat_send.at[n], lat_recv.at[2 * (n // 2) + par]),
            remote(high, dst.at[par], even_above, lat_send.at[n + 1], lat_recv.at[2 * (n // 2) + par]),
        ]

    def from_lat(dst, n):
        for p in range(2):
            remote(dst.at[p], dst.at[p], partner, lat_send.at[n + p], lat_recv.at[n + p]).wait_recv()

    def to_partner(src, dst, n):
        return remote(src, dst, partner, chip_send.at[n], chip_recv.at[n])

    place = lax.broadcasted_iota(jnp.int32, (rows, LANES), 0) * LANES + lax.broadcasted_iota(
        jnp.int32, (rows, LANES), 1
    )
    for g in (0, 2, 1):
        sl = pl.ds(g * rows, rows)
        weight = jnp.where(place < cnt[0, 0, g], 0.5 + vals[sl, :], 0.0)
        loads[sl, :] = weight
        loads[pl.ds(total_rows + g * rows, rows), :] = weight * vals[pl.ds(total_rows + g * rows, rows), :]
        loads[pl.ds(2 * total_rows + g * rows, rows), :] = weight * vals[pl.ds(2 * total_rows + g * rows, rows), :]
        c = cell[sl, :]
        if g == 1:
            index_a[sl, :] = stay_index(c, cr).astype(F32)
            index_b[sl, :] = (c & 255).astype(F32)
        else:
            index_a[sl, :] = side_index(c, cx - HALO if g == 0 else 0, cr).astype(F32)
            index_b[sl, :] = (c & 127).astype(F32)

    pl.semaphore_wait(barrier, 3 + len(peers))
    copies = [to_partner(vel, pv, 0), to_partner(frc, pf, 1), to_partner(bv, pb, 2)]
    copies += to_lat(vel.at[:, pl.ds(0, HALO)], vel.at[:, pl.ds(cx - HALO, HALO)], hv, 0)
    copies += to_lat(frc.at[:, pl.ds(0, 1)], frc.at[:, pl.ds(cx - 1, 1)], hf, 2)
    copies += to_lat(bv.at[pl.ds(0, HALO)], bv.at[pl.ds(cx - HALO, HALO)], hb, 4)
    for copy in copies:
        copy.start()

    step_rows = min(32, rows)
    acc_side[...] = jnp.zeros_like(acc_side)
    acc_s[...] = jnp.zeros_like(acc_s)
    bin_group(acc_side.at[0], loads, index_a, index_b, 0, rows, step_rows, 2, 8, total_rows)
    bin_group(acc_side.at[1], loads, index_a, index_b, 2 * rows, rows, step_rows, 2, 8, total_rows)
    sides = to_lat(acc_side.at[0], acc_side.at[1], got_a, 6) + [to_partner(acc_side.at[1 - par], got_c, 3)]
    for copy in sides:
        copy.start()
    bin_group(acc_s, loads, index_a, index_b, rows, rows, step_rows, 6, 16, total_rows)

    for q in range(3):
        for h in range(2):
            for s in range(HALO):
                row = q * 32 + (s * 2 + h) * 8
                lanes = pl.ds(h * LANES, LANES)
                edge_lo[pl.ds(row, 8), :] = jnp.zeros((8, LANES), F32)
                edge_hi[pl.ds(row, 8), :] = jnp.zeros((8, LANES), F32)
                for p in range(half):
                    base = q * half * SLOTS + p * SLOTS
                    edge_lo[pl.ds(row + p, 1), :] = acc_s[pl.ds(base + HALO + s, 1), lanes]
                    edge_hi[pl.ds(row + p, 1), :] = acc_s[pl.ds(base + HALO + cx - HALO + s, 1), lanes]
    late = to_lat(edge_lo, edge_hi, got_b, 8) + [to_partner(acc_s, got_s, 4)]
    for copy in late:
        copy.start()
    copies += sides + late

    field = rows_all * SLOTS

    def put(dst, c, parity, slot, value):
        dst[pl.ds(c * field + parity * cr * SLOTS + slot, cr, stride=SLOTS), :] = value

    near = par * (SLOTS - HALO)
    keep = jnp.where(l + par * (nl - 1) == par * 2 * (nl - 1), 0.0, 1.0)
    ext[...] = jnp.zeros_like(ext)
    for n in range(3):
        copies[n].wait_recv()
    for x in range(cx):
        put(bs, 0, par, x + HALO, bv[x])
        put(bs, 0, 1 - par, x + HALO, pb[x])
        for c in range(3):
            put(vs, c, par, x + HALO, vel[c, x])
            put(vs, c, 1 - par, x + HALO, pv[c, x])
            put(fs, c, par, x + HALO, frc[c, x])
            put(fs, c, 1 - par, x + HALO, pf[c, x])
    from_lat(hv, 0)
    from_lat(hf, 2)
    from_lat(hb, 4)
    for p in range(2):
        for s in range(HALO):
            put(bs, 0, p, near + s, hb[p, s])
            for c in range(3):
                put(vs, c, p, near + s, hv[p, c, s] * keep)
        for c in range(3):
            put(fs, c, p, 1 + par * (SLOTS - 3), hf[p, c, 0])

    def put_edge(ref, parity, slot, scale):
        for q in range(3):
            for h in range(2):
                for s in range(HALO):
                    value = ref[pl.ds(q * 32 + (s * 2 + h) * 8, half), :] * scale
                    start = q * field + (parity * cr + h) * SLOTS + slot + s
                    ext[pl.ds(start, half, stride=2 * SLOTS), :] = value

    from_lat(got_a, 6)
    for p in range(2):
        put_edge(got_a.at[p], p, HALO + par * (SLOTS - 3 * HALO), keep)
    sides[2].wait_recv()
    from_lat(got_b, 8)
    got_b[par] = got_b[par] + acc_side[par]
    got_b[1 - par] = got_b[1 - par] + got_c[...]
    for p in range(2):
        put_edge(got_b.at[p], p, near, 1.0)
    late[2].wait_recv()

    slot_of = lax.broadcasted_iota(jnp.int32, (SLOTS, LANES), 0)
    lane = lax.broadcasted_iota(jnp.int32, (WINDOW, LANES), 1)
    low = jnp.where(l == 0, HALO, 0)
    high = jnp.where(l == nl - 1, SLOTS - HALO, SLOTS)
    inside = jnp.where((slot_of >= low) & (slot_of < high), 1.0, 0.0)
    slot_here = lax.broadcasted_iota(jnp.int32, (WINDOW, LANES), 0) + window + 1
    inside_here = jnp.where((slot_here >= low) & (slot_here < high), 1.0, 0.0)
    is_south = lane == 0
    is_north = lane == LANES - 1

    def by_slot(R, c=0):
        return pl.ds((c * rows_all + R) * SLOTS, SLOTS)

    def near_slot(R, shift, c=0):
        return pl.ds((c * rows_all + R) * SLOTS + window + shift, WINDOW)

    def at(R, c=0):
        return pl.ds((c * rows_all + R) * WINDOW, WINDOW)

    def south(v):
        return jnp.where(is_south, 0.0, pltpu.roll(v, 1, 1))

    def north(v):
        return jnp.where(is_north, 0.0, pltpu.roll(v, LANES - 1, 1))

    for whose, ref in ((par, acc_s), (1 - par, got_s)):
        for r in range(cr):
            lanes = pl.ds((r & 1) * LANES, LANES)
            sums = []
            for q in range(3):
                more = ext[pl.ds(pl.multiple_of(q * field + (whose * cr + r) * SLOTS, 8), SLOTS), :]
                sums.append(ref[pl.ds((q * half + r // 2) * SLOTS, SLOTS), lanes] + more)
            inverse = 1.0 / (sums[0] + PRIOR_WEIGHT)
            basalt = sums[1] * inverse
            melt = sums[2] * inverse
            here = pl.ds(pl.multiple_of((whose * cr + r) * SLOTS, 8), SLOTS)
            mix[here, :] = basalt
            mix[pl.ds(pl.multiple_of(field + (whose * cr + r) * SLOTS, 8), SLOTS), :] = melt
            heavy = pl.ds(pl.multiple_of(2 * field + (whose * cr + r) * SLOTS, 8), SLOTS)
            fs[heavy, :] = fs[heavy, :] - BUOYANCY * basalt
            visc[here, :] = inside * (bs[here, :] * jnp.exp(CONTRAST_BASALT * basalt - CONTRAST_MELT * melt))

    weight_lo = jnp.where(kc == 0, 0.5 * RADIAL, RADIAL)
    weight_hi = jnp.where(kc == nc - 1, 0.5 * RADIAL, RADIAL)
    top = rows_all - 1
    v_at = [visc[near_slot(R, 1), :] for R in range(rows_all)]
    face = [weight_lo * v_at[0]]
    face += [0.5 * RADIAL * (v_at[R - 1] + v_at[R]) for R in range(1, rows_all)]
    face += [weight_hi * v_at[top]]
    face_ref = share
    for R in range(rows_all + 1):
        face_ref[pl.ds(R * WINDOW, WINDOW), :] = face[R]

    def below(R):
        return face_ref[pl.ds(R * WINDOW, WINDOW), :]

    def above(R):
        return below(R + 1)

    def diagonal(R):
        v = visc[near_slot(R, 1), :]
        scale = LATERAL * 0.5
        fw = scale * (v + visc[near_slot(R, 0), :])
        fe = scale * (v + visc[near_slot(R, 2), :])
        fs_, fn = scale * (v + south(v)), scale * (v + north(v))
        f_w[at(R), :] = fw
        f_e[at(R), :] = fe
        f_s[at(R), :] = fs_
        f_n[at(R), :] = fn
        return jnp.where(v > 0.0, fw + fe + fs_ + fn + below(R) + above(R), 1.0)

    u_low = u_high = m_low = m_high = None
    for n in range(cr):
        lo, hi = n, top - n
        p_low, p_high = diagonal(lo), diagonal(hi)
        if n > 0:
            p_low = p_low - below(lo) * u_low
            p_high = p_high - above(hi) * u_high
        i_low, i_high = 1.0 / p_low, 1.0 / p_high
        ip[at(lo), :] = i_low
        ip[at(hi), :] = i_high
        m_low = i_low if n == 0 else below(lo) * m_low * i_low
        m_high = i_high if n == 0 else above(hi) * m_high * i_high
        res0[at(lo), :] = m_low
        res1[at(hi), :] = m_high
        u_low, u_high = above(lo) * i_low, below(hi) * i_high
        up[at(lo), :] = u_low
        up[at(hi), :] = u_high
    middle = 1.0 / (1.0 - u_low * u_high)

    x0, y1 = m_low * middle, m_high * middle
    y0, x1 = u_high * x0, u_low * y1
    for n in range(cr - 1, -1, -1):
        lo, hi = n, top - n
        if n < cr - 1:
            x0 = res0[at(lo), :] + up[at(lo), :] * x0
            x1 = up[at(lo), :] * x1
            y0 = up[at(hi), :] * y0
            y1 = res1[at(hi), :] + up[at(hi), :] * y1
        res0[at(lo), :] = x0
        res1[at(lo), :] = x1
        res0[at(hi), :] = y0
        res1[at(hi), :] = y1

    def right_side(R, c):
        v = vs[near_slot(R, 1, c), :]
        return (
            fs[near_slot(R, 1, c), :]
            + f_w[at(R), :] * vs[near_slot(R, 0, c), :]
            + f_e[at(R), :] * vs[near_slot(R, 2, c), :]
            + f_s[at(R), :] * south(v)
            + f_n[at(R), :] * north(v)
        )

    def particular():
        low_m, high_m = [None] * 3, [None] * 3
        for n in range(cr):
            lo, hi = n, top - n
            for c in range(3):
                a, b = right_side(lo, c), right_side(hi, c)
                if n > 0:
                    a = a + below(lo) * low_m[c]
                    b = b + above(hi) * high_m[c]
                low_m[c] = a * ip[at(lo), :]
                high_m[c] = b * ip[at(hi), :]
                part[at(lo, c), :] = low_m[c]
                part[at(hi, c), :] = high_m[c]
        for c in range(3):
            x = (low_m[c] + u_low * high_m[c]) * middle
            y = high_m[c] + u_high * x
            part[at(cr - 1, c), :] = x
            part[at(cr, c), :] = y
            for n in range(cr - 2, -1, -1):
                lo, hi = n, top - n
                x = part[at(lo, c), :] + up[at(lo), :] * x
                y = part[at(hi, c), :] + up[at(hi), :] * y
                part[at(lo, c), :] = x
                part[at(hi, c), :] = y

    def gather(src, dst, phase):
        sent = []
        for d in (2, 1, 3):
            n = phase * (nc - 1) + d - 1
            sent.append(remote(src, dst.at[kc], peers[d - 1], rad_send.at[n], rad_recv.at[n]))
        for copy in sent:
            copy.start()
        dst[kc] = src[...]
        return sent

    def piece(source, i, number):
        return source[i, pl.ds(number * WINDOW, WINDOW), :]

    def solve(factors, source, first):
        sums = [piece(source, 0, first + 3 + c) for c in range(3)]
        fixed = [[piece(source, 0, first + c) for c in range(3)]]
        olds = [None]
        for i in range(1, nc):
            f = factors[i]
            olds.append([s * f["ih"] for s in sums])
            fixed.append([f["cf"] * piece(source, i, first + c) + f["cp"] * sums[c] for c in range(3)])
            sums = [piece(source, i, first + 3 + c) + f["e1"] * sums[c] + f["e2"] * fixed[i][c] for c in range(3)]
        for c in range(3):
            flux = None
            flux_hi[nc - 1, c] = jnp.zeros((WINDOW, LANES), F32)
            flux_lo[0, c] = jnp.zeros((WINDOW, LANES), F32)
            for i in range(nc - 1, 0, -1):
                f = factors[i]
                first_value = fixed[i][c] if flux is None else fixed[i][c] + f["f1"] * flux
                last_value = olds[i][c] + f["qq"] * first_value
                flux_lo[i, c] = f["fb"] * last_value + f["dl"] * first_value
                flux = f["fb"] * first_value - f["dl"] * last_value
                flux_hi[i - 1, c] = flux

    def solved(R, c):
        return part[at(R, c), :] + res0[at(R), :] * flux_lo[kc, c] + res1[at(R), :] * flux_hi[kc, c]

    particular()
    for number, value in enumerate(
        [res0[at(0), :], res1[at(0), :], res1[at(top), :], v_at[0], v_at[top]]
        + [part[at(0, c), :] for c in range(3)]
        + [part[at(top, c), :] for c in range(3)]
    ):
        snd1[pl.ds(number * WINDOW, WINDOW), :] = value
    sent = gather(snd1, rcv1, 0)
    copies += sent

    for c in range(2):
        for R in range(rows_all):
            fin[pl.ds((c * rows_all + R) * WINDOW, WINDOW), :] = mix[near_slot(R, 1, c), :]

    def give(n, fields, first):
        made = []
        for c in range(fields):
            theirs = pl.ds(pl.multiple_of(((first + c) * rows_all + (1 - par) * cr) * WINDOW, 8), cr * WINDOW)
            made.append(to_partner(fin.at[theirs], ret.at[first + c, pl.ds(0, cr * WINDOW)], n + c))
        for copy in made:
            copy.start()
        return made

    shared = give(5, 2, 0)
    for copy in shared:
        copy.wait_recv()
    copies += shared

    def collect(field, store):
        for i in range(1, 1 + cx // 2):
            mine = fin[pl.ds((field * rows_all + par * cr) * WINDOW + i, cr, stride=WINDOW), :]
            theirs = ret[field, pl.ds(i, cr, stride=WINDOW), :]
            store(par * (cx // 2) + i - 1, mine)
            store((1 - par) * (cx // 2) + i - 1, theirs)

    for c in range(2):
        collect(c, lambda x, value: comp.__setitem__((pl.ds(x * 2 * cr + c, cr, stride=2), slice(None)), value))
    for copy in sent:
        copy.wait_recv()

    factors = [None]
    slope = piece(rcv1, 0, 2)
    for i in range(1, nc):
        a, b, d, v_first = (piece(rcv1, i, n) for n in (0, 1, 2, 3))
        v_last = piece(rcv1, i - 1, 4)
        fb = 0.5 * RADIAL * (v_last + v_first)
        dl = 0.5 * RADIAL * (v_first - v_last)
        afb = a * fb
        h = 1.0 + slope * dl
        inverse_h = 1.0 / h
        inverse = 1.0 / (h * (1.0 - a * dl) - afb * (fb * slope))
        qq = fb * slope * inverse_h
        cf = h * inverse
        f1 = cf * b
        e2 = b * (fb * qq + dl)
        factors.append(dict(fb=fb, dl=dl, ih=inverse_h, qq=qq, cf=cf, cp=afb * inverse, f1=f1, e1=b * fb * inverse_h, e2=e2))
        slope = d + e2 * f1
    solve(factors, rcv1, 5)
    for c in range(3):
        for R in range(rows_all):
            vs[near_slot(R, 1, c), :] = solved(R, c) * inside_here

    particular()
    for c in range(3):
        snd2[pl.ds(c * WINDOW, WINDOW), :] = part[at(0, c), :]
        snd2[pl.ds((3 + c) * WINDOW, WINDOW), :] = part[at(top, c), :]
    sent = gather(snd2, rcv2, 1)
    for copy in sent:
        copy.wait_recv()
    copies += sent
    solve(factors, rcv2, 0)
    for c in range(3):
        for R in range(rows_all):
            fin[pl.ds(((2 + c) * rows_all + R) * WINDOW, WINDOW), :] = solved(R, c)
    shared = give(7, 3, 2)
    for copy in shared:
        copy.wait_recv()
    copies += shared
    for c in range(3):
        collect(2 + c, lambda x, value: out.__setitem__((c, x), value))
    for copy in copies:
        copy.wait_send()


def solution(mesh):
    nl, nk = mesh.shape["lat"], mesh.shape["rad"]

    def local(tracer_values, tracer_cell, tracer_count, base_viscosity, velocity, forcing):
        cx, cr, ny = base_viscosity.shape
        slots = tracer_cell.shape[2]
        assert nk == 8 and cx + 2 * HALO == SLOTS and ny == LANES and cr == 12
        total_rows = slots // LANES
        vmem = functools.partial(pltpu.VMEM, dtype=F32)
        field = 2 * cr * SLOTS
        compact = 2 * cr * WINDOW
        spare = 8 * SLOTS
        nc = nk // 2
        scratch = [
            vmem((3 * total_rows, LANES)), vmem((total_rows, LANES)), vmem((total_rows, LANES)),
            vmem((3 * (cr // 2) * SLOTS, 2 * LANES)), vmem((2, 96, LANES)), vmem((96, LANES)), vmem((96, LANES)),
            vmem((2, 96, LANES)), vmem((2, 96, LANES)), vmem((96, LANES)), vmem((3 * (cr // 2) * SLOTS, 2 * LANES)),
            vmem((2, 3, HALO, cr, LANES)), vmem((2, 3, 1, cr, LANES)), vmem((2, HALO, cr, LANES)),
            vmem((3, cx, cr, LANES)), vmem((3, cx, cr, LANES)), vmem((cx, cr, LANES)),
            vmem((3 * field + 2 * spare, LANES)), vmem((3 * field + spare, LANES)), vmem((3 * field + spare, LANES)),
            vmem((field + spare, LANES)), vmem((field, LANES)),
        ]
        scratch += [vmem((compact, LANES))] * 8 + [vmem((3 * compact, LANES)), vmem((2 * field, LANES))]
        scratch += [vmem((Q1, LANES)), vmem((nc, Q1, LANES)), vmem((Q2, LANES)), vmem((nc, Q2, LANES))]
        scratch += [vmem((nc, 3, WINDOW, LANES))] * 2 + [vmem((compact + WINDOW, LANES))]
        scratch += [vmem((5 * compact + spare, LANES)), vmem((5, cr * WINDOW + 8 * WINDOW, LANES))]
        scratch += [pltpu.SemaphoreType.DMA((n,)) for n in (10, 10, 10, 10, 2 * (nc - 1), 2 * (nc - 1))]
        v = pl.BlockSpec(memory_space=pltpu.VMEM)
        smoothed, composition = pl.pallas_call(
            functools.partial(kernel, nl, nk),
            out_shape=[
                jax.ShapeDtypeStruct((3, cx, cr, ny), F32),
                jax.ShapeDtypeStruct((cx * cr * 2, ny), F32),
            ],
            in_specs=[v, v, pl.BlockSpec(memory_space=pltpu.SMEM), v, v, v],
            out_specs=[v, v],
            scratch_shapes=scratch,
            compiler_params=pltpu.CompilerParams(collective_id=0, has_side_effects=True),
        )(
            tracer_values.reshape(3 * total_rows, LANES),
            tracer_cell.reshape(total_rows, LANES),
            tracer_count,
            base_viscosity,
            velocity,
            forcing,
        )
        return smoothed, jnp.transpose(composition.reshape(cx, cr, 2, ny), (2, 0, 1, 3))

    return jax.shard_map(
        local,
        mesh=mesh,
        in_specs=(
            P("lat", "rad", None, None),
            P("lat", "rad", None),
            P("lat", "rad", None),
            P("lat", "rad", None),
            P(None, "lat", "rad", None),
            P(None, "lat", "rad", None),
        ),
        out_specs=(P(None, "lat", "rad", None), P(None, "lat", "rad", None)),
        check_vma=False,
    )
```

time: 45.8 us -> 41.8 us (0.913)
  Pallas kernels: 42.2 us -> 38.6 us
    pallas_call x1, Pallas kernels: 42.2 us -> 38.6 us  [local(): pl.pallas_call(functools.partial(kernel, nl, nk), out_shape=[jax.ShapeDty...]
    transpose x2 -> x0, local copies, waits for them, and re-layouts: 1 us -> none  [the longest x1 0.99 us: local(): jnp.transpose(smoothed[:, :, own], (0, 2, 1, 3))]
    unnamed x4, local copies, waits for them, and re-layouts: 1.7 us -> 2.4 us
where the time goes in v2:
time: 41.8 us; the launch traced here: 41.7 us
  Pallas kernels  38.6 us (92%)
  local copies, waits for them, and re-layouts  2.4 us (6%)
  between operations  0.65 us (2%)
    pallas_call x1, Pallas kernels, local(): pl.pallas_call(functools.partial(kernel, nl, nk), out_shape=[jax.ShapeDty...  38.6 us
    unnamed x4, local copies, waits for them, and re-layouts  2.4 us

profile of v2, /device:TPU:1, one launch (start us, length us, event | category | flops | bytes accessed | tf_op | source)
XLA Modules:
  0.0 41.7 jit_solution(2379993911284093253)
XLA Ops:
  0.6 38.6 %shard_map.77 = (f32[3,12,12,128]{3,2,1,0:T(8,128)}, f32[288,128]{1,0:T(8,128)}) custom-call(f32[1152,128]{1,0:T(8,128)} %bitcast.5, s32[384,128]{1,0:T(8,128)} %bitcast.6, s32[1,1,3]{2,1,0:T(1,128)} %cnt.1, f32[12,12,128]{2,1,0:T(8,128)} %bv.1, f32[3,12,12,128]{3,2,1,0:T(8,128)} %vel.1, f32[3,12,12,128]{3,2,1,0:T(8,128)} %frc.1), custom_call_target="tpu_custom_call" | custom-call | tf_op jit(solution)/shard_map/pallas_call | solution.py:512
  39.3 0.0 copy-start
  39.3 1.7 %copy.10 = f32[3,12,12,128]{3,2,1,0:T(8,128)} copy(f32[3,12,12,128]{3,2,1,0:T(8,128)} %get-tuple-element.8) | data formatting | bytes 442368
  41.0 0.0 copy-done
  41.0 0.7 %copy.11 = f32[2,12,12,128]{3,0,2,1:T(2,128)} copy(f32[2,12,12,128]{3,0,2,1:T(2,128)S(1)} %bitcast.7) | data formatting | bytes 294912
Async XLA Ops:
  39.3 1.7 %copy-start = (f32[288,128]{1,0:T(8,128)S(1)}, f32[288,128]{1,0:T(8,128)}, u32[]{:S(2)}) copy-start(f32[288,128]{1,0:T(8,128)} %get-tuple-element.5) | copy-start | bytes 442372

commit v3 on v2

--- a/solution.py
+++ b/solution.py
@@ -99,10 +99,19 @@
     peers = [(l, 2 * lax.rem(kc + d, nc) + par) for d in range(1, nc)]
     window = par * 6
 
+    has_below = l > 0
+    has_above = l < nl - 1
+    has_beside = l != par * (nl - 1)
+
     barrier = pltpu.get_barrier_semaphore()
     beside = lm + par * (lp - lm)
-    for device in [(beside, 2 * kc), (beside, 2 * kc + 1), partner] + peers:
+    for device in [partner] + peers:
         pl.semaphore_signal(barrier, inc=1, device_id=device, device_id_type=MESH)
+
+    @pl.when(has_beside)
+    def _():
+        for p in range(2):
+            pl.semaphore_signal(barrier, inc=1, device_id=(beside, 2 * kc + p), device_id_type=MESH)
 
     def remote(src, dst, device, send, recv):
         return pltpu.make_async_remote_copy(
@@ -111,16 +120,26 @@
 
     def to_lat(low, high, dst, n):
         return [
-            remote(low, dst.at[par], odd_below, lat_send.at[n], lat_recv.at[2 * (n // 2) + par]),
-            remote(high, dst.at[par], even_above, lat_send.at[n + 1], lat_recv.at[2 * (n // 2) + par]),
+            (has_below, remote(low, dst.at[par], odd_below, lat_send.at[n], lat_recv.at[n + par])),
+            (has_above, remote(high, dst.at[par], even_above, lat_send.at[n + 1], lat_recv.at[n + par])),
         ]
 
-    def from_lat(dst, n):
-        for p in range(2):
-            remote(dst.at[p], dst.at[p], partner, lat_send.at[n + p], lat_recv.at[n + p]).wait_recv()
+    def start(entries):
+        for condition, copy in entries:
+            if condition is None:
+                copy.start()
+            else:
+                pl.when(condition)(copy.start)
+
+    def from_lat(pairs):
+        @pl.when(has_beside)
+        def _():
+            for dst, n in pairs:
+                for p in range(2):
+                    remote(dst.at[p], dst.at[p], partner, lat_send.at[n + p], lat_recv.at[n + p]).wait_recv()
 
     def to_partner(src, dst, n):
-        return remote(src, dst, partner, chip_send.at[n], chip_recv.at[n])
+        return (None, remote(src, dst, partner, chip_send.at[n], chip_recv.at[n]))
 
     place = lax.broadcasted_iota(jnp.int32, (rows, LANES), 0) * LANES + lax.broadcasted_iota(
         jnp.int32, (rows, LANES), 1
@@ -139,13 +158,12 @@
             index_a[sl, :] = side_index(c, cx - HALO if g == 0 else 0, cr).astype(F32)
             index_b[sl, :] = (c & 127).astype(F32)
 
-    pl.semaphore_wait(barrier, 3 + len(peers))
+    pl.semaphore_wait(barrier, 1 + len(peers) + jnp.where(has_below, 1, 0) + jnp.where(has_above, 1, 0))
     copies = [to_partner(vel, pv, 0), to_partner(frc, pf, 1), to_partner(bv, pb, 2)]
     copies += to_lat(vel.at[:, pl.ds(0, HALO)], vel.at[:, pl.ds(cx - HALO, HALO)], hv, 0)
     copies += to_lat(frc.at[:, pl.ds(0, 1)], frc.at[:, pl.ds(cx - 1, 1)], hf, 2)
     copies += to_lat(bv.at[pl.ds(0, HALO)], bv.at[pl.ds(cx - HALO, HALO)], hb, 4)
-    for copy in copies:
-        copy.start()
+    start(copies)
 
     step_rows = min(32, rows)
     acc_side[...] = jnp.zeros_like(acc_side)
@@ -153,8 +171,7 @@
     bin_group(acc_side.at[0], loads, index_a, index_b, 0, rows, step_rows, 2, 8, total_rows)
     bin_group(acc_side.at[1], loads, index_a, index_b, 2 * rows, rows, step_rows, 2, 8, total_rows)
     sides = to_lat(acc_side.at[0], acc_side.at[1], got_a, 6) + [to_partner(acc_side.at[1 - par], got_c, 3)]
-    for copy in sides:
-        copy.start()
+    start(sides)
     bin_group(acc_s, loads, index_a, index_b, rows, rows, step_rows, 6, 16, total_rows)
 
     for q in range(3):
@@ -169,8 +186,7 @@
                     edge_lo[pl.ds(row + p, 1), :] = acc_s[pl.ds(base + HALO + s, 1), lanes]
                     edge_hi[pl.ds(row + p, 1), :] = acc_s[pl.ds(base + HALO + cx - HALO + s, 1), lanes]
     late = to_lat(edge_lo, edge_hi, got_b, 8) + [to_partner(acc_s, got_s, 4)]
-    for copy in late:
-        copy.start()
+    start(late)
     copies += sides + late
 
     field = rows_all * SLOTS
@@ -179,10 +195,13 @@
         dst[pl.ds(c * field + parity * cr * SLOTS + slot, cr, stride=SLOTS), :] = value
 
     near = par * (SLOTS - HALO)
-    keep = jnp.where(l + par * (nl - 1) == par * 2 * (nl - 1), 0.0, 1.0)
+
+    def kept(value):
+        return jnp.where(has_beside, value, 0.0)
+
     ext[...] = jnp.zeros_like(ext)
     for n in range(3):
-        copies[n].wait_recv()
+        copies[n][1].wait_recv()
     for x in range(cx):
         put(bs, 0, par, x + HALO, bv[x])
         put(bs, 0, 1 - par, x + HALO, pb[x])
@@ -191,43 +210,42 @@
             put(vs, c, 1 - par, x + HALO, pv[c, x])
             put(fs, c, par, x + HALO, frc[c, x])
             put(fs, c, 1 - par, x + HALO, pf[c, x])
-    from_lat(hv, 0)
-    from_lat(hf, 2)
-    from_lat(hb, 4)
+    from_lat([(hv, 0), (hf, 2), (hb, 4)])
     for p in range(2):
         for s in range(HALO):
-            put(bs, 0, p, near + s, hb[p, s])
+            put(bs, 0, p, near + s, kept(hb[p, s]))
             for c in range(3):
-                put(vs, c, p, near + s, hv[p, c, s] * keep)
+                put(vs, c, p, near + s, kept(hv[p, c, s]))
         for c in range(3):
-            put(fs, c, p, 1 + par * (SLOTS - 3), hf[p, c, 0])
-
-    def put_edge(ref, parity, slot, scale):
+            put(fs, c, p, 1 + par * (SLOTS - 3), kept(hf[p, c, 0]))
+
+    def put_edge(ref, parity, slot):
         for q in range(3):
             for h in range(2):
                 for s in range(HALO):
-                    value = ref[pl.ds(q * 32 + (s * 2 + h) * 8, half), :] * scale
+                    value = ref[pl.ds(q * 32 + (s * 2 + h) * 8, half), :]
                     start = q * field + (parity * cr + h) * SLOTS + slot + s
                     ext[pl.ds(start, half, stride=2 * SLOTS), :] = value
 
-    from_lat(got_a, 6)
+    from_lat([(got_a, 6)])
     for p in range(2):
-        put_edge(got_a.at[p], p, HALO + par * (SLOTS - 3 * HALO), keep)
-    sides[2].wait_recv()
-    from_lat(got_b, 8)
-    got_b[par] = got_b[par] + acc_side[par]
-    got_b[1 - par] = got_b[1 - par] + got_c[...]
+        got_a[p] = kept(got_a[p])
+        put_edge(got_a.at[p], p, HALO + par * (SLOTS - 3 * HALO))
+    sides[2][1].wait_recv()
+    from_lat([(got_b, 8)])
+    got_b[par] = kept(got_b[par]) + acc_side[par]
+    got_b[1 - par] = kept(got_b[1 - par]) + got_c[...]
     for p in range(2):
-        put_edge(got_b.at[p], p, near, 1.0)
-    late[2].wait_recv()
+        put_edge(got_b.at[p], p, near)
+    late[2][1].wait_recv()
 
     slot_of = lax.broadcasted_iota(jnp.int32, (SLOTS, LANES), 0)
     lane = lax.broadcasted_iota(jnp.int32, (WINDOW, LANES), 1)
     low = jnp.where(l == 0, HALO, 0)
     high = jnp.where(l == nl - 1, SLOTS - HALO, SLOTS)
-    inside = jnp.where((slot_of >= low) & (slot_of < high), 1.0, 0.0)
+    inside = (slot_of >= low) & (slot_of < high)
     slot_here = lax.broadcasted_iota(jnp.int32, (WINDOW, LANES), 0) + window + 1
-    inside_here = jnp.where((slot_here >= low) & (slot_here < high), 1.0, 0.0)
+    inside_here = (slot_here >= low) & (slot_here < high)
     is_south = lane == 0
     is_north = lane == LANES - 1
 
@@ -261,7 +279,9 @@
             mix[pl.ds(pl.multiple_of(field + (whose * cr + r) * SLOTS, 8), SLOTS), :] = melt
             heavy = pl.ds(pl.multiple_of(2 * field + (whose * cr + r) * SLOTS, 8), SLOTS)
             fs[heavy, :] = fs[heavy, :] - BUOYANCY * basalt
-            visc[here, :] = inside * (bs[here, :] * jnp.exp(CONTRAST_BASALT * basalt - CONTRAST_MELT * melt))
+            visc[here, :] = jnp.where(
+                inside, bs[here, :] * jnp.exp(CONTRAST_BASALT * basalt - CONTRAST_MELT * melt), 0.0
+            )
 
     weight_lo = jnp.where(kc == 0, 0.5 * RADIAL, RADIAL)
     weight_hi = jnp.where(kc == nc - 1, 0.5 * RADIAL, RADIAL)
@@ -364,9 +384,8 @@
         sent = []
         for d in (2, 1, 3):
             n = phase * (nc - 1) + d - 1
-            sent.append(remote(src, dst.at[kc], peers[d - 1], rad_send.at[n], rad_recv.at[n]))
-        for copy in sent:
-            copy.start()
+            sent.append((None, remote(src, dst.at[kc], peers[d - 1], rad_send.at[n], rad_recv.at[n])))
+        start(sent)
         dst[kc] = src[...]
         return sent
 
@@ -416,13 +435,12 @@
         for c in range(fields):
             theirs = pl.ds(pl.multiple_of(((first + c) * rows_all + (1 - par) * cr) * WINDOW, 8), cr * WINDOW)
             made.append(to_partner(fin.at[theirs], ret.at[first + c, pl.ds(0, cr * WINDOW)], n + c))
-        for copy in made:
-            copy.start()
+        start(made)
         return made
 
     shared = give(5, 2, 0)
     for copy in shared:
-        copy.wait_recv()
+        copy[1].wait_recv()
     copies += shared
 
     def collect(field, store):
@@ -435,7 +453,7 @@
     for c in range(2):
         collect(c, lambda x, value: comp.__setitem__((pl.ds(x * 2 * cr + c, cr, stride=2), slice(None)), value))
     for copy in sent:
-        copy.wait_recv()
+        copy[1].wait_recv()
 
     factors = [None]
     slope = piece(rcv1, 0, 2)
@@ -457,7 +475,7 @@
     solve(factors, rcv1, 5)
     for c in range(3):
         for R in range(rows_all):
-            vs[near_slot(R, 1, c), :] = solved(R, c) * inside_here
+            vs[near_slot(R, 1, c), :] = jnp.where(inside_here, solved(R, c), 0.0)
 
     particular()
     for c in range(3):
@@ -465,7 +483,7 @@
         snd2[pl.ds((3 + c) * WINDOW, WINDOW), :] = part[at(top, c), :]
     sent = gather(snd2, rcv2, 1)
     for copy in sent:
-        copy.wait_recv()
+        copy[1].wait_recv()
     copies += sent
     solve(factors, rcv2, 0)
     for c in range(3):
@@ -473,12 +491,15 @@
             fin[pl.ds(((2 + c) * rows_all + R) * WINDOW, WINDOW), :] = solved(R, c)
     shared = give(7, 3, 2)
     for copy in shared:
-        copy.wait_recv()
+        copy[1].wait_recv()
     copies += shared
     for c in range(3):
         collect(2 + c, lambda x, value: out.__setitem__((c, x), value))
-    for copy in copies:
-        copy.wait_send()
+    for condition, copy in copies:
+        if condition is None:
+            copy.wait_send()
+        else:
+            pl.when(condition)(copy.wait_send)
 
 
 def solution(mesh):

time: 41.8 us -> 33.2 us (0.79)
  Pallas kernels: 38.6 us -> 29.6 us
    pallas_call x1, Pallas kernels: 38.6 us -> 29.6 us  [local(): pl.pallas_call(functools.partial(kernel, nl, nk), out_shape=[jax.ShapeDty...]
where the time goes in v3:
time: 33.2 us; the launch traced here: 32.7 us
  Pallas kernels  29.6 us (89%)
  local copies, waits for them, and re-layouts  2.4 us (7%)
  between operations  0.65 us (2%)
    pallas_call x1, Pallas kernels, local(): pl.pallas_call(functools.partial(kernel, nl, nk), out_shape=[jax.ShapeDty...  29.6 us
    unnamed x4, local copies, waits for them, and re-layouts  2.4 us

profile of v3, /device:TPU:1, one launch (start us, length us, event | category | flops | bytes accessed | tf_op | source)
XLA Modules:
  0.0 32.7 jit_solution(7546683206188685576)
XLA Ops:
  0.6 29.6 %shard_map.77 = (f32[3,12,12,128]{3,2,1,0:T(8,128)}, f32[288,128]{1,0:T(8,128)}) custom-call(f32[1152,128]{1,0:T(8,128)} %bitcast.5, s32[384,128]{1,0:T(8,128)} %bitcast.6, s32[1,1,3]{2,1,0:T(1,128)} %cnt.1, f32[12,12,128]{2,1,0:T(8,128)} %bv.1, f32[3,12,12,128]{3,2,1,0:T(8,128)} %vel.1, f32[3,12,12,128]{3,2,1,0:T(8,128)} %frc.1), custom_call_target="tpu_custom_call" | custom-call | tf_op jit(solution)/shard_map/pallas_call | solution.py:533
  30.3 0.0 copy-start
  30.3 1.7 %copy.10 = f32[3,12,12,128]{3,2,1,0:T(8,128)} copy(f32[3,12,12,128]{3,2,1,0:T(8,128)} %get-tuple-element.8) | data formatting | bytes 442368
  32.0 0.0 copy-done
  32.0 0.7 %copy.11 = f32[2,12,12,128]{3,0,2,1:T(2,128)} copy(f32[2,12,12,128]{3,0,2,1:T(2,128)S(1)} %bitcast.7) | data formatting | bytes 294912
Async XLA Ops:
  30.3 1.7 %copy-start = (f32[288,128]{1,0:T(8,128)S(1)}, f32[288,128]{1,0:T(8,128)}, u32[]{:S(2)}) copy-start(f32[288,128]{1,0:T(8,128)} %get-tuple-element.5) | copy-start | bytes 442372

commit v4 on v3

--- a/solution.py
+++ b/solution.py
@@ -31,7 +31,7 @@
     rows = (cell >> 7) - first_plane * cr
     plane = (rows >= cr).astype(jnp.int32)
     radial = rows - cr * plane
-    return (plane * 2 + (radial & 1)) * 8 + (radial >> 1)
+    return (plane * 2 + (radial & 1)) * (cr // 2) + (radial >> 1)
 
 
 def stay_index(cell, cr):
@@ -74,8 +74,8 @@
 
 
 def kernel(
-    nl, nk, vals, cell, cnt, bv, vel, frc, out, comp,
-    loads, index_a, index_b, acc_s, acc_side, edge_lo, edge_hi, got_a, got_b, got_c, got_s,
+    nl, nk, vals_in, cell_in, cnt, bv_in, vel_in, frc_in, out, comp,
+    vals, cell, bv, vel, frc, load_sem, loads, index_a, index_b, acc_s, acc_side, edge_lo, edge_hi, got_a, got_b, got_c, got_s,
     hv, hf, hb, pv, pf, pb,
     ext, vs, fs, bs, visc, f_w, f_e, f_s, f_n, up, ip, res0, res1, part, mix,
     snd1, rcv1, snd2, rcv2, flux_lo, flux_hi, share, fin, ret,
@@ -103,6 +103,21 @@
     has_above = l < nl - 1
     has_beside = l != par * (nl - 1)
 
+    loading = {}
+    for g in (0, 2, 1):
+        pairs = [(cell_in, cell, g * rows)] + [(vals_in, vals, q * total_rows + g * rows) for q in range(3)]
+        loading[g] = [
+            pltpu.make_async_copy(src.at[pl.ds(row, rows)], dst.at[pl.ds(row, rows)], load_sem.at[4 * g + n])
+            for n, (src, dst, row) in enumerate(pairs)
+        ]
+    loading[3] = [
+        pltpu.make_async_copy(src, dst, load_sem.at[12 + n])
+        for n, (src, dst) in enumerate([(bv_in, bv), (vel_in, vel), (frc_in, frc)])
+    ]
+    for copies in loading.values():
+        for copy in copies:
+            copy.start()
+
     barrier = pltpu.get_barrier_semaphore()
     beside = lm + par * (lp - lm)
     for device in [partner] + peers:
@@ -144,7 +159,13 @@
     place = lax.broadcasted_iota(jnp.int32, (rows, LANES), 0) * LANES + lax.broadcasted_iota(
         jnp.int32, (rows, LANES), 1
     )
-    for g in (0, 2, 1):
+    step_rows = min(32, rows)
+    acc_side[...] = jnp.zeros_like(acc_side)
+    acc_s[...] = jnp.zeros_like(acc_s)
+
+    def prepare(g):
+        for copy in loading[g]:
+            copy.wait()
         sl = pl.ds(g * rows, rows)
         weight = jnp.where(place < cnt[0, 0, g], 0.5 + vals[sl, :], 0.0)
         loads[sl, :] = weight
@@ -158,29 +179,28 @@
             index_a[sl, :] = side_index(c, cx - HALO if g == 0 else 0, cr).astype(F32)
             index_b[sl, :] = (c & 127).astype(F32)
 
+    prepare(0)
+    bin_group(acc_side.at[0], loads, index_a, index_b, 0, rows, step_rows, 2, 8, total_rows)
+
     pl.semaphore_wait(barrier, 1 + len(peers) + jnp.where(has_below, 1, 0) + jnp.where(has_above, 1, 0))
-    copies = [to_partner(vel, pv, 0), to_partner(frc, pf, 1), to_partner(bv, pb, 2)]
-    copies += to_lat(vel.at[:, pl.ds(0, HALO)], vel.at[:, pl.ds(cx - HALO, HALO)], hv, 0)
-    copies += to_lat(frc.at[:, pl.ds(0, 1)], frc.at[:, pl.ds(cx - 1, 1)], hf, 2)
-    copies += to_lat(bv.at[pl.ds(0, HALO)], bv.at[pl.ds(cx - HALO, HALO)], hb, 4)
+    copies = [to_partner(vel_in, pv, 0), to_partner(frc_in, pf, 1), to_partner(bv_in, pb, 2)]
+    copies += to_lat(vel_in.at[:, pl.ds(0, HALO)], vel_in.at[:, pl.ds(cx - HALO, HALO)], hv, 0)
+    copies += to_lat(frc_in.at[:, pl.ds(0, 1)], frc_in.at[:, pl.ds(cx - 1, 1)], hf, 2)
+    copies += to_lat(bv_in.at[pl.ds(0, HALO)], bv_in.at[pl.ds(cx - HALO, HALO)], hb, 4)
     start(copies)
 
-    step_rows = min(32, rows)
-    acc_side[...] = jnp.zeros_like(acc_side)
-    acc_s[...] = jnp.zeros_like(acc_s)
-    bin_group(acc_side.at[0], loads, index_a, index_b, 0, rows, step_rows, 2, 8, total_rows)
+    prepare(2)
     bin_group(acc_side.at[1], loads, index_a, index_b, 2 * rows, rows, step_rows, 2, 8, total_rows)
     sides = to_lat(acc_side.at[0], acc_side.at[1], got_a, 6) + [to_partner(acc_side.at[1 - par], got_c, 3)]
     start(sides)
+    prepare(1)
     bin_group(acc_s, loads, index_a, index_b, rows, rows, step_rows, 6, 16, total_rows)
 
     for q in range(3):
         for h in range(2):
             for s in range(HALO):
-                row = q * 32 + (s * 2 + h) * 8
+                row = (q * 4 + s * 2 + h) * half
                 lanes = pl.ds(h * LANES, LANES)
-                edge_lo[pl.ds(row, 8), :] = jnp.zeros((8, LANES), F32)
-                edge_hi[pl.ds(row, 8), :] = jnp.zeros((8, LANES), F32)
                 for p in range(half):
                     base = q * half * SLOTS + p * SLOTS
                     edge_lo[pl.ds(row + p, 1), :] = acc_s[pl.ds(base + HALO + s, 1), lanes]
@@ -200,6 +220,8 @@
         return jnp.where(has_beside, value, 0.0)
 
     ext[...] = jnp.zeros_like(ext)
+    for copy in loading[3]:
+        copy.wait()
     for n in range(3):
         copies[n][1].wait_recv()
     for x in range(cx):
@@ -219,24 +241,26 @@
         for c in range(3):
             put(fs, c, p, 1 + par * (SLOTS - 3), kept(hf[p, c, 0]))
 
-    def put_edge(ref, parity, slot):
+    def put_edge(ref, block, parity, slot):
         for q in range(3):
             for h in range(2):
                 for s in range(HALO):
-                    value = ref[pl.ds(q * 32 + (s * 2 + h) * 8, half), :]
+                    value = ref[pl.ds(q * block + (s * 2 + h) * half, half), :]
                     start = q * field + (parity * cr + h) * SLOTS + slot + s
                     ext[pl.ds(start, half, stride=2 * SLOTS), :] = value
 
     from_lat([(got_a, 6)])
     for p in range(2):
         got_a[p] = kept(got_a[p])
-        put_edge(got_a.at[p], p, HALO + par * (SLOTS - 3 * HALO))
+        put_edge(got_a.at[p], 32, p, HALO + par * (SLOTS - 3 * HALO))
     sides[2][1].wait_recv()
     from_lat([(got_b, 8)])
-    got_b[par] = kept(got_b[par]) + acc_side[par]
-    got_b[1 - par] = kept(got_b[1 - par]) + got_c[...]
+    for q in range(3):
+        theirs, mine = pl.ds(q * 4 * half, 4 * half), pl.ds(q * 32, 4 * half)
+        got_b[par, theirs] = kept(got_b[par, theirs]) + acc_side[par, mine]
+        got_b[1 - par, theirs] = kept(got_b[1 - par, theirs]) + got_c[mine]
     for p in range(2):
-        put_edge(got_b.at[p], p, near)
+        put_edge(got_b.at[p], 4 * half, p, near)
     late[2][1].wait_recv()
 
     slot_of = lax.broadcasted_iota(jnp.int32, (SLOTS, LANES), 0)
@@ -516,9 +540,11 @@
         spare = 8 * SLOTS
         nc = nk // 2
         scratch = [
+            vmem((3 * total_rows, LANES)), pltpu.VMEM((total_rows, LANES), jnp.int32), vmem((cx, cr, LANES)),
+            vmem((3, cx, cr, LANES)), vmem((3, cx, cr, LANES)), pltpu.SemaphoreType.DMA((15,)),
             vmem((3 * total_rows, LANES)), vmem((total_rows, LANES)), vmem((total_rows, LANES)),
-            vmem((3 * (cr // 2) * SLOTS, 2 * LANES)), vmem((2, 96, LANES)), vmem((96, LANES)), vmem((96, LANES)),
-            vmem((2, 96, LANES)), vmem((2, 96, LANES)), vmem((96, LANES)), vmem((3 * (cr // 2) * SLOTS, 2 * LANES)),
+            vmem((3 * (cr // 2) * SLOTS, 2 * LANES)), vmem((2, 96, LANES)), vmem((72, LANES)), vmem((72, LANES)),
+            vmem((2, 96, LANES)), vmem((2, 72, LANES)), vmem((96, LANES)), vmem((3 * (cr // 2) * SLOTS, 2 * LANES)),
             vmem((2, 3, HALO, cr, LANES)), vmem((2, 3, 1, cr, LANES)), vmem((2, HALO, cr, LANES)),
             vmem((3, cx, cr, LANES)), vmem((3, cx, cr, LANES)), vmem((cx, cr, LANES)),
             vmem((3 * field + 2 * spare, LANES)), vmem((3 * field + spare, LANES)), vmem((3 * field + spare, LANES)),
@@ -530,13 +556,14 @@
         scratch += [vmem((5 * compact + spare, LANES)), vmem((5, cr * WINDOW + 8 * WINDOW, LANES))]
         scratch += [pltpu.SemaphoreType.DMA((n,)) for n in (10, 10, 10, 10, 2 * (nc - 1), 2 * (nc - 1))]
         v = pl.BlockSpec(memory_space=pltpu.VMEM)
+        h = pl.BlockSpec(memory_space=pltpu.HBM)
         smoothed, composition = pl.pallas_call(
             functools.partial(kernel, nl, nk),
             out_shape=[
-                jax.ShapeDtypeStruct((3, cx, cr, ny), F32),
-                jax.ShapeDtypeStruct((cx * cr * 2, ny), F32),
+                pltpu.VMEM((3, cx, cr, ny), F32),
+                pltpu.VMEM((cx * cr * 2, ny), F32),
             ],
-            in_specs=[v, v, pl.BlockSpec(memory_space=pltpu.SMEM), v, v, v],
+            in_specs=[h, h, pl.BlockSpec(memory_space=pltpu.SMEM), h, h, h],
             out_specs=[v, v],
             scratch_shapes=scratch,
             compiler_params=pltpu.CompilerParams(collective_id=0, has_side_effects=True),

time: 33.2 us -> 30.1 us (0.907)
  the two profiles are of different devices: /device:TPU:1 before, /device:TPU:9 now
where the time goes in v4:
time: 30.1 us; the launch traced here: 30 us
  Pallas kernels  27.9 us (93%)
  local copies, waits for them, and re-layouts  1.38 us (5%)
  between operations  0.64 us (2%)
    pallas_call x1, Pallas kernels, local(): pl.pallas_call(functools.partial(kernel, nl, nk), out_shape=[pltpu.VMEM((...  27.9 us
    unnamed x2, local copies, waits for them, and re-layouts  1.38 us

profile of v4, /device:TPU:9, one launch (start us, length us, event | category | flops | bytes accessed | tf_op | source)
XLA Modules:
  0.0 30.0 jit_solution(740401764164896565)
XLA Ops:
  0.6 27.9 %shard_map.77 = (f32[3,12,12,128]{3,2,1,0:T(8,128)S(1)}, f32[288,128]{1,0:T(8,128)S(1)}) custom-call(f32[1152,128]{1,0:T(8,128)} %bitcast.6, s32[384,128]{1,0:T(8,128)} %bitcast.7, s32[1,1,3]{2,1,0:T(1,128)} %cnt.1, f32[12,12,128]{2,1,0:T(8,128)} %bv_in.1, f32[3,12,12,128]{3,2,1,0:T(8,128)} %vel_in.1, f32[3,12,12,128]{3,2,1,0:T(8,128)} %frc_in.1), custom_call_target="tpu_custom_call" | custom-call | tf_op jit(solution)/shard_map/pallas_call | solution.py:560
  28.6 0.7 %copy.10 = f32[3,12,12,128]{3,2,1,0:T(8,128)} copy(f32[3,12,12,128]{3,2,1,0:T(8,128)S(1)} %get-tuple-element.6) | data formatting | bytes 442368
  29.3 0.7 %copy.11 = f32[2,12,12,128]{3,0,2,1:T(2,128)} copy(f32[2,12,12,128]{3,0,2,1:T(2,128)S(1)} %bitcast.5) | data formatting | bytes 294912

commit v5 on v4

--- a/solution.py
+++ b/solution.py
@@ -74,8 +74,8 @@
 
 
 def kernel(
-    nl, nk, vals_in, cell_in, cnt, bv_in, vel_in, frc_in, out, comp,
-    vals, cell, bv, vel, frc, load_sem, loads, index_a, index_b, acc_s, acc_side, edge_lo, edge_hi, got_a, got_b, got_c, got_s,
+    nl, nk, vals_in, cell_in, cnt_in, bv_in, vel_in, frc_in, out, comp,
+    cnt, vals, cell, bv, vel, frc, load_sem, loads, index_a, index_b, acc_s, acc_side, edge_lo, edge_hi, got_a, got_b, got_c, got_s,
     hv, hf, hb, pv, pf, pb,
     ext, vs, fs, bs, visc, f_w, f_e, f_s, f_n, up, ip, res0, res1, part, mix,
     snd1, rcv1, snd2, rcv2, flux_lo, flux_hi, share, fin, ret,
@@ -103,7 +103,7 @@
     has_above = l < nl - 1
     has_beside = l != par * (nl - 1)
 
-    loading = {}
+    loading = {4: [pltpu.make_async_copy(cnt_in, cnt, load_sem.at[15])]}
     for g in (0, 2, 1):
         pairs = [(cell_in, cell, g * rows)] + [(vals_in, vals, q * total_rows + g * rows) for q in range(3)]
         loading[g] = [
@@ -179,6 +179,7 @@
             index_a[sl, :] = side_index(c, cx - HALO if g == 0 else 0, cr).astype(F32)
             index_b[sl, :] = (c & 127).astype(F32)
 
+    loading[4][0].wait()
     prepare(0)
     bin_group(acc_side.at[0], loads, index_a, index_b, 0, rows, step_rows, 2, 8, total_rows)
 
@@ -194,7 +195,7 @@
     sides = to_lat(acc_side.at[0], acc_side.at[1], got_a, 6) + [to_partner(acc_side.at[1 - par], got_c, 3)]
     start(sides)
     prepare(1)
-    bin_group(acc_s, loads, index_a, index_b, rows, rows, step_rows, 6, 16, total_rows)
+    bin_group(acc_s, loads, index_a, index_b, rows, rows, min(64, rows), 6, 16, total_rows)
 
     for q in range(3):
         for h in range(2):
@@ -404,13 +405,13 @@
                 part[at(lo, c), :] = x
                 part[at(hi, c), :] = y
 
-    def gather(src, dst, phase):
+    def gather(src, dst, phase, where):
         sent = []
         for d in (2, 1, 3):
             n = phase * (nc - 1) + d - 1
-            sent.append((None, remote(src, dst.at[kc], peers[d - 1], rad_send.at[n], rad_recv.at[n])))
+            sent.append((None, remote(src.at[where], dst.at[kc, where], peers[d - 1], rad_send.at[n], rad_recv.at[n])))
         start(sent)
-        dst[kc] = src[...]
+        dst[kc, where] = src[where]
         return sent
 
     def piece(source, i, number):
@@ -440,14 +441,14 @@
     def solved(R, c):
         return part[at(R, c), :] + res0[at(R), :] * flux_lo[kc, c] + res1[at(R), :] * flux_hi[kc, c]
 
+    for number, value in enumerate([res0[at(0), :], res1[at(0), :], res1[at(top), :], v_at[0], v_at[top]]):
+        snd1[pl.ds(number * WINDOW, WINDOW), :] = value
+    sent = gather(snd1, rcv1, 2, pl.ds(0, 5 * WINDOW))
     particular()
-    for number, value in enumerate(
-        [res0[at(0), :], res1[at(0), :], res1[at(top), :], v_at[0], v_at[top]]
-        + [part[at(0, c), :] for c in range(3)]
-        + [part[at(top, c), :] for c in range(3)]
-    ):
-        snd1[pl.ds(number * WINDOW, WINDOW), :] = value
-    sent = gather(snd1, rcv1, 0)
+    for c in range(3):
+        snd1[pl.ds((5 + c) * WINDOW, WINDOW), :] = part[at(0, c), :]
+        snd1[pl.ds((8 + c) * WINDOW, WINDOW), :] = part[at(top, c), :]
+    sent += gather(snd1, rcv1, 0, pl.ds(5 * WINDOW, 6 * WINDOW))
     copies += sent
 
     for c in range(2):
@@ -505,7 +506,7 @@
     for c in range(3):
         snd2[pl.ds(c * WINDOW, WINDOW), :] = part[at(0, c), :]
         snd2[pl.ds((3 + c) * WINDOW, WINDOW), :] = part[at(top, c), :]
-    sent = gather(snd2, rcv2, 1)
+    sent = gather(snd2, rcv2, 1, pl.ds(0, Q2))
     for copy in sent:
         copy[1].wait_recv()
     copies += sent
@@ -540,8 +541,9 @@
         spare = 8 * SLOTS
         nc = nk // 2
         scratch = [
+            pltpu.SMEM((1, 1, 3), jnp.int32),
             vmem((3 * total_rows, LANES)), pltpu.VMEM((total_rows, LANES), jnp.int32), vmem((cx, cr, LANES)),
-            vmem((3, cx, cr, LANES)), vmem((3, cx, cr, LANES)), pltpu.SemaphoreType.DMA((15,)),
+            vmem((3, cx, cr, LANES)), vmem((3, cx, cr, LANES)), pltpu.SemaphoreType.DMA((16,)),
             vmem((3 * total_rows, LANES)), vmem((total_rows, LANES)), vmem((total_rows, LANES)),
             vmem((3 * (cr // 2) * SLOTS, 2 * LANES)), vmem((2, 96, LANES)), vmem((72, LANES)), vmem((72, LANES)),
             vmem((2, 96, LANES)), vmem((2, 72, LANES)), vmem((96, LANES)), vmem((3 * (cr // 2) * SLOTS, 2 * LANES)),
@@ -554,7 +556,7 @@
         scratch += [vmem((Q1, LANES)), vmem((nc, Q1, LANES)), vmem((Q2, LANES)), vmem((nc, Q2, LANES))]
         scratch += [vmem((nc, 3, WINDOW, LANES))] * 2 + [vmem((compact + WINDOW, LANES))]
         scratch += [vmem((5 * compact + spare, LANES)), vmem((5, cr * WINDOW + 8 * WINDOW, LANES))]
-        scratch += [pltpu.SemaphoreType.DMA((n,)) for n in (10, 10, 10, 10, 2 * (nc - 1), 2 * (nc - 1))]
+        scratch += [pltpu.SemaphoreType.DMA((n,)) for n in (10, 10, 10, 10, 3 * (nc - 1), 3 * (nc - 1))]
         v = pl.BlockSpec(memory_space=pltpu.VMEM)
         h = pl.BlockSpec(memory_space=pltpu.HBM)
         smoothed, composition = pl.pallas_call(
@@ -563,7 +565,7 @@
                 pltpu.VMEM((3, cx, cr, ny), F32),
                 pltpu.VMEM((cx * cr * 2, ny), F32),
             ],
-            in_specs=[h, h, pl.BlockSpec(memory_space=pltpu.SMEM), h, h, h],
+            in_specs=[h] * 6,
             out_specs=[v, v],
             scratch_shapes=scratch,
             compiler_params=pltpu.CompilerParams(collective_id=0, has_side_effects=True),

time: 30.1 us -> 29.1 us (0.967)
  the two profiles are of different devices: /device:TPU:9 before, /device:TPU:1 now
where the time goes in v5:
time: 29.1 us; the launch traced here: 28.6 us
  Pallas kernels  26.6 us (91%)
  local copies, waits for them, and re-layouts  1.38 us (5%)
  between operations  0.64 us (2%)
    pallas_call x1, Pallas kernels, local(): pl.pallas_call(functools.partial(kernel, nl, nk), out_shape=[pltpu.VMEM((...  26.6 us
    unnamed x2, local copies, waits for them, and re-layouts  1.38 us

profile of v5, /device:TPU:1, one launch (start us, length us, event | category | flops | bytes accessed | tf_op | source)
XLA Modules:
  0.0 28.6 jit_solution(2092794319782360092)
XLA Ops:
  0.6 26.6 %shard_map.77 = (f32[3,12,12,128]{3,2,1,0:T(8,128)S(1)}, f32[288,128]{1,0:T(8,128)S(1)}) custom-call(f32[1152,128]{1,0:T(8,128)} %bitcast.6, s32[384,128]{1,0:T(8,128)} %bitcast.7, s32[1,1,3]{2,1,0:T(1,128)} %cnt_in.1, f32[12,12,128]{2,1,0:T(8,128)} %bv_in.1, f32[3,12,12,128]{3,2,1,0:T(8,128)} %vel_in.1, f32[3,12,12,128]{3,2,1,0:T(8,128)} %frc_in.1), custom_call_target="tpu_custom_call" | custom-call | tf_op jit(solution)/shard_map/pallas_call | solution.py:562
  27.2 0.7 %copy.10 = f32[3,12,12,128]{3,2,1,0:T(8,128)} copy(f32[3,12,12,128]{3,2,1,0:T(8,128)S(1)} %get-tuple-element.6) | data formatting | bytes 442368
  27.9 0.7 %copy.11 = f32[2,12,12,128]{3,0,2,1:T(2,128)} copy(f32[2,12,12,128]{3,0,2,1:T(2,128)S(1)} %bitcast.5) | data formatting | bytes 294912

commit v6 on v5

--- a/solution.py
+++ b/solution.py
@@ -46,7 +46,7 @@
     return [index == (base + 16.0 * t).astype(BF16) for t in range(tiles)]
 
 
-def bin_group(acc, loads, index_a, index_b, first_row, rows, step_rows, tiles_a, tiles_b, total_rows):
+def bin_groups(acc, loads, index_a, index_b, first_rows, steps, step_rows, tiles_a, tiles_b, total_rows):
     zero = jnp.zeros((16, LANES), BF16)
     one = jnp.ones((16, LANES), BF16)
 
@@ -56,12 +56,16 @@
     def body(step, carry):
         left, right = [], []
         for j in range(step_rows):
-            row = first_row + step * step_rows + j
-            values = [spread(loads, q * total_rows + row) for q in range(3)]
-            hot_a = hot_masks(spread(index_a, row), tiles_a)
-            hot_b = hot_masks(spread(index_b, row), tiles_b)
-            left.append(jnp.concatenate([jnp.where(h, v, zero) for v in values for h in hot_a], 0))
-            right.append(jnp.concatenate([jnp.where(h, one, zero) for h in hot_b], 0))
+            tall, wide = [], []
+            for first_row in first_rows:
+                row = first_row + step * step_rows + j
+                values = [spread(loads, q * total_rows + row) for q in range(3)]
+                hot_a = hot_masks(spread(index_a, row), tiles_a)
+                hot_b = hot_masks(spread(index_b, row), tiles_b)
+                tall += [jnp.where(h, v, zero) for v in values for h in hot_a]
+                wide += [jnp.where(h, one, zero) for h in hot_b]
+            left.append(jnp.concatenate(tall, 0))
+            right.append(jnp.concatenate(wide, 0))
         acc[...] += lax.dot_general(
             jnp.concatenate(left, 1),
             jnp.concatenate(right, 1),
@@ -70,12 +74,12 @@
         )
         return carry
 
-    lax.fori_loop(0, rows // step_rows, body, 0)
+    lax.fori_loop(steps[0], steps[1], body, 0)
 
 
 def kernel(
     nl, nk, vals_in, cell_in, cnt_in, bv_in, vel_in, frc_in, out, comp,
-    cnt, vals, cell, bv, vel, frc, load_sem, loads, index_a, index_b, acc_s, acc_side, edge_lo, edge_hi, got_a, got_b, got_c, got_s,
+    cnt, vals, cell, bv, vel, frc, load_sem, loads, index_a, index_b, acc_s, acc_pair, acc_side, edge_lo, edge_hi, got_a, got_b, got_c, got_s,
     hv, hf, hb, pv, pf, pb,
     ext, vs, fs, bs, visc, f_w, f_e, f_s, f_n, up, ip, res0, res1, part, mix,
     snd1, rcv1, snd2, rcv2, flux_lo, flux_hi, share, fin, ret,
@@ -160,7 +164,7 @@
         jnp.int32, (rows, LANES), 1
     )
     step_rows = min(32, rows)
-    acc_side[...] = jnp.zeros_like(acc_side)
+    acc_pair[...] = jnp.zeros_like(acc_pair)
     acc_s[...] = jnp.zeros_like(acc_s)
 
     def prepare(g):
@@ -181,7 +185,13 @@
 
     loading[4][0].wait()
     prepare(0)
-    bin_group(acc_side.at[0], loads, index_a, index_b, 0, rows, step_rows, 2, 8, total_rows)
+    prepare(2)
+    steps = rows // step_rows
+
+    def bin_pair(begin, end):
+        bin_groups(acc_pair, loads, index_a, index_b, (0, 2 * rows), (begin, end), step_rows, 2, 8, total_rows)
+
+    bin_pair(0, steps // 2)
 
     pl.semaphore_wait(barrier, 1 + len(peers) + jnp.where(has_below, 1, 0) + jnp.where(has_above, 1, 0))
     copies = [to_partner(vel_in, pv, 0), to_partner(frc_in, pf, 1), to_partner(bv_in, pb, 2)]
@@ -190,12 +200,14 @@
     copies += to_lat(bv_in.at[pl.ds(0, HALO)], bv_in.at[pl.ds(cx - HALO, HALO)], hb, 4)
     start(copies)
 
-    prepare(2)
-    bin_group(acc_side.at[1], loads, index_a, index_b, 2 * rows, rows, step_rows, 2, 8, total_rows)
+    bin_pair(steps // 2, steps)
+    for g in range(2):
+        acc_side[g] = acc_pair[pl.ds(g * 96, 96), pl.ds(g * LANES, LANES)]
     sides = to_lat(acc_side.at[0], acc_side.at[1], got_a, 6) + [to_partner(acc_side.at[1 - par], got_c, 3)]
     start(sides)
     prepare(1)
-    bin_group(acc_s, loads, index_a, index_b, rows, rows, min(64, rows), 6, 16, total_rows)
+    long_rows = min(64, rows)
+    bin_groups(acc_s, loads, index_a, index_b, (rows,), (0, rows // long_rows), long_rows, 6, 16, total_rows)
 
     for q in range(3):
         for h in range(2):
@@ -545,7 +557,7 @@
             vmem((3 * total_rows, LANES)), pltpu.VMEM((total_rows, LANES), jnp.int32), vmem((cx, cr, LANES)),
             vmem((3, cx, cr, LANES)), vmem((3, cx, cr, LANES)), pltpu.SemaphoreType.DMA((16,)),
             vmem((3 * total_rows, LANES)), vmem((total_rows, LANES)), vmem((total_rows, LANES)),
-            vmem((3 * (cr // 2) * SLOTS, 2 * LANES)), vmem((2, 96, LANES)), vmem((72, LANES)), vmem((72, LANES)),
+            vmem((3 * (cr // 2) * SLOTS, 2 * LANES)), vmem((192, 2 * LANES)), vmem((2, 96, LANES)), vmem((72, LANES)), vmem((72, LANES)),
             vmem((2, 96, LANES)), vmem((2, 72, LANES)), vmem((96, LANES)), vmem((3 * (cr // 2) * SLOTS, 2 * LANES)),
             vmem((2, 3, HALO, cr, LANES)), vmem((2, 3, 1, cr, LANES)), vmem((2, HALO, cr, LANES)),
             vmem((3, cx, cr, LANES)), vmem((3, cx, cr, LANES)), vmem((cx, cr, LANES)),

time: 29.1 us -> 28.7 us (0.986)
  Pallas kernels: 26.6 us -> 26.2 us
    pallas_call x1, Pallas kernels: 26.6 us -> 26.2 us  [local(): pl.pallas_call(functools.partial(kernel, nl, nk), out_shape=[pltpu.VMEM((...]
where the time goes in v6:
time: 28.7 us; the launch traced here: 28.2 us
  Pallas kernels  26.2 us (91%)
  local copies, waits for them, and re-layouts  1.38 us (5%)
  between operations  0.64 us (2%)
    pallas_call x1, Pallas kernels, local(): pl.pallas_call(functools.partial(kernel, nl, nk), out_shape=[pltpu.VMEM((...  26.2 us
    unnamed x2, local copies, waits for them, and re-layouts  1.38 us

profile of v6, /device:TPU:1, one launch (start us, length us, event | category | flops | bytes accessed | tf_op | source)
XLA Modules:
  0.0 28.2 jit_solution(2178784179367450271)
XLA Ops:
  0.6 26.2 %shard_map.77 = (f32[3,12,12,128]{3,2,1,0:T(8,128)S(1)}, f32[288,128]{1,0:T(8,128)S(1)}) custom-call(f32[1152,128]{1,0:T(8,128)} %bitcast.6, s32[384,128]{1,0:T(8,128)} %bitcast.7, s32[1,1,3]{2,1,0:T(1,128)} %cnt_in.1, f32[12,12,128]{2,1,0:T(8,128)} %bv_in.1, f32[3,12,12,128]{3,2,1,0:T(8,128)} %vel_in.1, f32[3,12,12,128]{3,2,1,0:T(8,128)} %frc_in.1), custom_call_target="tpu_custom_call" | custom-call | tf_op jit(solution)/shard_map/pallas_call | solution.py:574
  26.8 0.7 %copy.10 = f32[3,12,12,128]{3,2,1,0:T(8,128)} copy(f32[3,12,12,128]{3,2,1,0:T(8,128)S(1)} %get-tuple-element.6) | data formatting | bytes 442368
  27.5 0.7 %copy.11 = f32[2,12,12,128]{3,0,2,1:T(2,128)} copy(f32[2,12,12,128]{3,0,2,1:T(2,128)S(1)} %bitcast.5) | data formatting | bytes 294912
